TPU v7x, 256 devices: a whole 4x4x8 slice. The times are simulated.
256 devices in a mesh: req: 32 (over y, x, core), wgt: 8 (over z).
Axes of the slice: x: 4, y: 4, z: 8, core: 2. Of those that a mesh axis runs over, the one named last changes fastest.
Arguments:
- arrivals: bfloat16 [128, 48, 6144], P('req', None, 'wgt'), may hold values from -6 to 6
- group_of: int32 [128], replicated, may hold values from 0 to 31, as said below
- lengths: int32 [128], P('req'), may hold values from 1 to 2048, as said below
- page_table: int32 [128, 16], P('req'), may hold values from 0 to 39, as said below
- ln_gain: bfloat16 [6144], replicated, may hold values from 0.25 to 1.75
- ln_bias: bfloat16 [6144], replicated, may hold values from -1.5 to 1.5
- w_qkv: bfloat16 [6144, 9216], P('req', 'wgt'), may hold values from -0.078125 to 0.078125
- qkv_bias: bfloat16 [9216], P('wgt'), may hold values from -4.5 to 4.5
- key_pool: bfloat16 [1280, 128, 3072], P('req', None, 'wgt'), may hold values from -8 to 8
- value_pool: bfloat16 [1280, 128, 3072], P('req', None, 'wgt'), may hold values from -6 to 6
Outputs:
- attended: bfloat16 [128, 48, 3072], P('req', None, 'wgt')
- new_keys: bfloat16 [128, 48, 3072], P('req', None, 'wgt')
- new_values: bfloat16 [128, 48, 3072], P('req', None, 'wgt')
Inputs may be any that keep to these rules, and one draw needn't show every extreme that they name: `group_of`: every group number is named by exactly 4 requests; the requests that arrive at one group (consecutive blocks of 4 in arrival order) name different groups. `lengths`: in each group at most one request has more than 1024 cached tokens; some request has exactly 2048. `page_table`: entries name pages of the request's group's own pool of 40; the pages that hold cached tokens of one group's requests are all different.
All inputs are finite; a program needn't handle non-finite values.
Results may differ from a plain program's by a relative error of at most 0.0066.
Values may be sent and summed in bfloat16 or wider, within the bound.
A program may use at most 128 MiB of HBM per device.

v0:
```python
import math

import jax
import jax.numpy as jnp
from jax import lax
from jax.sharding import PartitionSpec as P

HEAD = 96
ROT = 24


EPS = 1e-05


def rotary(block, positions):
    half_rot = ROT // 2
    inverse = jnp.power(10000.0, -jnp.arange(half_rot, dtype=jnp.float32) * 2.0 / ROT)
    angles = positions[:, :, None] * inverse[None, None, :]
    cosine = jnp.cos(angles)[:, :, None, :]
    sine = jnp.sin(angles)[:, :, None, :]
    first = block[..., :half_rot]
    second = block[..., half_rot:ROT]
    return jnp.concatenate(
        [first * cosine - second * sine, second * cosine + first * sine, block[..., ROT:]], axis=-1
    )


def per_device(
    arrivals, group_of, lengths, page_table, ln_gain, ln_bias, w_qkv, qkv_bias, key_pool, value_pool
):
    req_count = lengths.shape[0]
    fresh_len = arrivals.shape[1]
    model_width = ln_gain.shape[0]
    local_cols = w_qkv.shape[1]
    local_heads = local_cols // (3 * HEAD)
    everyone = group_of.shape[0]
    my_group = lax.axis_index("req")
    same_group = group_of[:, None] == group_of[None, :]
    earlier = jnp.arange(everyone)[None, :] < jnp.arange(everyone)[:, None]
    rank_in = jnp.sum((same_group & earlier).astype(jnp.int32), axis=1)
    wanted = (group_of[None, :] == my_group) & (rank_in[None, :] == jnp.arange(req_count)[:, None])
    chooser = wanted.astype(jnp.bfloat16)
    all_lengths = lax.all_gather(lengths, "req", axis=0, tiled=True)
    arrival_ids = my_group * req_count + jnp.arange(req_count, dtype=jnp.int32)
    assigned = group_of[arrival_ids] * req_count + rank_in[arrival_ids]
    gathered = lax.all_gather(arrivals, "wgt", axis=2, tiled=True)
    widened = gathered.astype(jnp.float32)
    center = jnp.mean(widened, axis=-1, keepdims=True)
    spread = jnp.mean(jnp.square(widened - center), axis=-1, keepdims=True)
    normed = (widened - center) * lax.rsqrt(spread + EPS) * ln_gain.astype(
        jnp.float32
    ) + ln_bias.astype(jnp.float32)
    project_normed = normed.astype(jnp.bfloat16).reshape(req_count * fresh_len, model_width)
    summed = jnp.dot(
        project_normed,
        lax.all_gather(w_qkv, "req", axis=0, tiled=True),
        preferred_element_type=jnp.float32,
    )
    summed = summed + qkv_bias.astype(jnp.float32)
    projected = summed.reshape(req_count, fresh_len, local_heads, 3, HEAD)
    positions = (
        all_lengths[assigned][:, None] + jnp.arange(fresh_len, dtype=jnp.int32)[None, :]
    ).astype(jnp.float32)
    queries = rotary(projected[:, :, :, 0], positions)
    turned = rotary(projected[:, :, :, 1], positions)
    stacked = jnp.stack([queries, turned, projected[:, :, :, 2]], axis=3)
    local_packed = stacked.astype(jnp.bfloat16).reshape(req_count, fresh_len, local_cols)
    packed = jnp.einsum(
        "jr,rcd->jcd",
        chooser,
        lax.all_gather(local_packed, "req", axis=0, tiled=True),
        preferred_element_type=jnp.float32,
    ).astype(jnp.bfloat16)
    triple = packed.reshape(req_count, fresh_len, local_heads, 3, HEAD)
    queries = triple[:, :, :, 0]
    fresh_keys = triple[:, :, :, 1]
    fresh_values = triple[:, :, :, 2]
    span = page_table.shape[1] * key_pool.shape[1]
    cached_keys = key_pool[page_table].reshape(req_count, span, local_heads, HEAD)
    cached_values = value_pool[page_table].reshape(req_count, span, local_heads, HEAD)
    scale = 1.0 / math.sqrt(HEAD)
    scores_old = (
        jnp.einsum("rqhd,rkhd->rhqk", queries, cached_keys, preferred_element_type=jnp.float32)
        * scale
    )
    visible = jnp.arange(span, dtype=jnp.int32)[None, None, None, :] < lengths[:, None, None, None]
    scores_old = jnp.where(visible, scores_old, -1e30)
    scores_new = (
        jnp.einsum("rqhd,rkhd->rhqk", queries, fresh_keys, preferred_element_type=jnp.float32)
        * scale
    )
    causal = jnp.arange(fresh_len)[:, None] >= jnp.arange(fresh_len)[None, :]
    scores_new = jnp.where(causal[None, None, :, :], scores_new, -1e30)
    peak = jnp.maximum(
        jnp.max(scores_old, axis=-1, keepdims=True), jnp.max(scores_new, axis=-1, keepdims=True)
    )
    exp_old = jnp.exp(scores_old - peak)
    exp_new = jnp.exp(scores_new - peak)
    denom = jnp.sum(exp_old, axis=-1, keepdims=True) + jnp.sum(exp_new, axis=-1, keepdims=True)
    weight_old = (exp_old / denom).astype(jnp.bfloat16)
    weight_new = (exp_new / denom).astype(jnp.bfloat16)
    mixed = jnp.einsum(
        "rhqk,rkhd->rqhd", weight_old, cached_values, preferred_element_type=jnp.float32
    )
    mixed = mixed + jnp.einsum(
        "rhqk,rkhd->rqhd", weight_new, fresh_values, preferred_element_type=jnp.float32
    )
    attended = mixed.astype(jnp.bfloat16).reshape(req_count, fresh_len, local_heads * HEAD)
    return (
        attended,
        fresh_keys.reshape(req_count, fresh_len, local_heads * HEAD),
        fresh_values.reshape(req_count, fresh_len, local_heads * HEAD),
    )


def solution(mesh):
    in_specs = (
        P("req", None, "wgt"),
        P(),
        P("req"),
        P("req", None),
        P(),
        P(),
        P("req", "wgt"),
        P("wgt"),
        P("req", None, "wgt"),
        P("req", None, "wgt"),
    )
    out_specs = (P("req", None, "wgt"), P("req", None, "wgt"), P("req", None, "wgt"))
    return jax.shard_map(
        per_device, mesh=mesh, in_specs=in_specs, out_specs=out_specs, check_vma=False
    )
```

profile of v0, /device:TPU:1, one launch (start us, length us, event | category | flops | bytes accessed | tf_op | source)
XLA Modules:
  0.0 250.1 jit_solution(2974459212197650404)
XLA Ops:
  7.2 0.0 all-gather.4.cloned.1.call-start
  7.2 0.7 all-gather.4.cloned.1.call-update
  7.9 0.0 all-gather.6.cloned.1.call-start
  7.9 0.7 all-gather.6.cloned.1.call-update
  8.7 0.0 all-gather.8.cloned.1.call-start
  8.7 0.7 convert_element_type.48
  9.4 0.7 convert_element_type.49
  10.1 0.7 convert_element_type.51
  10.8 1.3 gather_fusion.1
  12.1 0.9 convert_reduce_fusion.1
  13.0 0.6 gather_fusion.2
  13.7 1.3 dynamic-slice
  15.6 0.9 dynamic-update-slice
  16.5 14.5 %all-reduce = s32[128]{0:T(128)S(1)} all-reduce(s32[128]{0:T(128)S(1)} %dynamic-update-slice), channel_id=1, replica_groups=mesh['req'=32,'wgt'=8] {'req'}, use_global_device_ids=true, to_apply=%add | all-reduce | flops 128 | bytes 1024
  31.0 0.6 gather_fusion.3
  31.6 0.1 add_convert_fusion.2
  31.7 0.4 multiply_cosine_fusion
  32.1 20.2 %all-gather.4.cloned.1.call-done = bf16[4,48,6144]{2,1,0:T(8,128)(2,1)} async-done(((bf16[4,48,768]{2,1,0:T(8,128)(2,1)}), bf16[4,48,6144]{2,1,0:T(8,128)(2,1)}) %all-gather.4.cloned.1.call-update) | async-done | bytes 2359312 | tf_op jit(solution)/shard_map/all_gather | solution.py:46
  52.4 2.2 convert_reduce_fusion
  54.6 2.4 fusion.10
  57.0 0.0 copy-done.1
  57.0 1.0 fusion.13
  58.1 70.1 %all-gather.6.cloned.1.call-done = bf16[6144,1152]{1,0:T(8,128)(2,1)} async-done(((bf16[192,1152]{1,0:T(8,128)(2,1)}), bf16[6144,1152]{1,0:T(8,128)(2,1)}) %all-gather.6.cloned.1.call-update) | async-done | bytes 14155792 | tf_op jit(solution)/shard_map/all_gather | solution.py:56
  128.2 6.8 %convolution_add_fusion = f32[192,1152]{1,0:T(8,128)S(1)} fusion(bf16[192,6144]{1,0:T(8,128)(2,1)S(1)} %bitcast.51, bf16[6144,1152]{1,0:T(8,128)(2,1)} %all-gather.6.cloned.1.call-done, f32[1152]{0:T(1024)S(1)} %convert_element_type.51), kind=kOutput, calls=%fused_computation.29 | convolution fusion | flops 2718130176 | bytes 17404416 | tf_op jit(solution)/shard_map/dot_general | solution.py:54
  135.1 1.5 reshape.167
  136.6 0.0 copy-start.2
  136.6 0.6 fusion.38
  137.2 0.4 slice.86
  137.6 0.2 slice.87
  137.8 0.2 slice.88
  138.0 0.7 subtract_convert_fusion.1
  138.6 0.9 maximum_bitcast_fusion
  139.5 0.4 copy.80
  139.9 0.4 copy.81
  140.3 1.6 pad_maximum_fusion
  142.0 1.5 convert_element_type.53
  143.4 0.0 all-gather.8.cloned.1.call-update
  143.5 0.0 copy-done.2
  143.5 0.1 reshape.173
  143.6 6.2 %gather_fusion.4 = bf16[64,128,384]{2,1,0:T(8,128)(2,1)} fusion(bf16[40,128,384]{2,1,0:T(8,128)(2,1)} %param.18, s32[1024]{0:T(1024)S(1)} %pad_clamp_fusion), kind=kCustom, calls=%fused_computation.4 | custom fusion | bytes 12583168 | tf_op jit(solution)/shard_map/gather | solution.py:79
  149.8 16.0 %reshape.224 = bf16[4,2048,4,96]{3,2,1,0:T(4,128)(2,1)} reshape(bf16[64,128,384]{2,1,0:T(8,128)(2,1)} %gather_fusion.4) | data formatting | bytes 12582912 | tf_op jit(solution)/shard_map/reshape | solution.py:79
  165.8 6.2 %gather_fusion = bf16[64,128,384]{2,1,0:T(8,128)(2,1)} fusion(bf16[40,128,384]{2,1,0:T(8,128)(2,1)} %param.19, s32[1024]{0:T(1024)S(1)} %pad_clamp_fusion), kind=kCustom, calls=%fused_computation | custom fusion | bytes 12583168 | tf_op jit(solution)/shard_map/gather | solution.py:80
  172.0 16.1 %reshape.223 = bf16[4,2048,4,96]{3,2,1,0:T(4,128)(2,1)} reshape(bf16[64,128,384]{2,1,0:T(8,128)(2,1)} %gather_fusion) | data formatting | bytes 12582912 | tf_op jit(solution)/shard_map/reshape | solution.py:80
  188.1 0.0 copy-done
  188.1 0.1 iota_compare_fusion.1
  188.2 26.5 %all-gather.8.cloned.1.call-done = bf16[128,48,1152]{2,1,0:T(8,128)(2,1)} async-done(((bf16[4,48,1152]{2,1,0:T(8,128)(2,1)}), bf16[128,48,1152]{2,1,0:T(8,128)(2,1)}) %all-gather.8.cloned.1.call-update) | async-done | bytes 14155792 | tf_op jit(solution)/shard_map/all_gather | solution.py:71
  214.8 9.3 %fusion.19 = bf16[4,48,1152]{2,0,1:T(4,128)(2,1)S(1)} fusion(bf16[128,48,1152]{2,1,0:T(8,128)(2,1)} %all-gather.8.cloned.1.call-done, s32[128]{0:T(128)S(1)} %convert_reduce_fusion.1, pred[128]{0:T(512)(128)(4,1)S(1)} %broadcast_compare_fusion), kind=kOutput, calls=%fused_computation.30 | convolution fusion | flops 56845312 | bytes 14598784 | tf_op jit(solution)/shard_map/jr,rcd->jcd/dot_general | solution.py:68
  224.0 0.9 reshape.225
  225.0 3.0 %slice_reduce_fusion = (bf16[4,48,4,96]{3,2,0,1:T(4,128)(2,1)S(1)}, bf16[4,48,4,96]{3,2,0,1:T(4,128)(2,1)S(1)}, bf16[4,48,4,1,96]{4,3,2,0,1:T(2,128)(2,1)S(1)}, ...) fusion(bf16[4,48,4,3,96]{4,3,2,0,1:T(4,128)(2,1)S(1)} %reshape.225), kind=kLoop, calls=%fused_computation.81 | loop fusion | bytes 1179648 | tf_op jit(solution)/shard_map/slice | solution.py:77
  228.0 0.0 slice-start
  228.0 0.3 fusion.39
  228.3 0.0 slice-start.1
  228.3 7.6 %fusion.8 = (f32[4,4,48]{2,1,0:T(4,128)S(1)}, f32[4,4,48,2048]{3,2,1,0:T(8,128)S(1)}) fusion(pred[4,2048]{1,0:T(4,128)(4,1)S(1)} %iota_compare_fusion.1, bf16[4,2048,4,96]{3,2,1,0:T(4,128)(2,1)} %reshape.224, bf16[4,48,4,1,96]{4,3,2,0,1:T(2,128)(2,1)S(1)} %get-tuple-element.8), kind=kOutput, calls=%fused_computation.18 | convolution fusion | flops 306707712 | bytes 12741632 | tf_op jit(solution)/shard_map/rqhd,rkhd->rhqk/dot_general | solution.py:83
  235.9 0.1 fusion.25
  236.0 1.5 fusion.9
  237.5 0.0 slice-done
  237.5 3.1 %fusion.4 = f32[4,4,96,48]{2,3,1,0:T(8,128)S(1)} fusion(bf16[4,2048,4,96]{3,2,1,0:T(4,128)(2,1)S(1)} %bitcast.46, f32[4,4,48,2048]{3,2,1,0:T(8,128)S(1)} %get-tuple-element.19, f32[4,4,48]{2,1,0:T(4,128)S(1)} %add.131, f32[4,4,48]{2,1,0:T(4,128)S(1)} %max.8, pred[4,2048]{1,0:T(4,128)(4,1)S(1)} %iota_compare_fusion.1), kind=kOutput, calls=%fused_computation.9 | convolution fusion | flops 309854208 | bytes 12892160 | tf_op jit(solution)/shard_map/rhqk,rkhd->rqhd/dot_general | solution.py:102
  240.7 0.3 fusion.24
  241.0 0.1 copy.91
  241.0 0.8 reshape.170
  241.9 0.2 reshape.226
  242.1 0.7 copy.110
  242.7 0.2 reshape.227
  242.9 0.7 copy.112
  (20 shorter events, 0.1 us)
Async XLA Ops:
  7.2 45.2 %all-gather.4.cloned.1.call-start = ((), (), s32[]{:S(2)}) async-start(), calls=%async_computation | async-start | bytes 2654208 | tf_op jit(solution)/shard_map/all_gather | solution.py:46
  7.9 120.3 %all-gather.6.cloned.1.call-start = ((), (), s32[]{:S(2)}) async-start(), calls=%async_computation.1 | async-start | bytes 14598144 | tf_op jit(solution)/shard_map/all_gather | solution.py:56
  8.7 206.1 %all-gather.8.cloned.1.call-start = ((), (), s32[]{:S(2)}) async-start(), calls=%async_computation.2 | async-start | bytes 14598144 | tf_op jit(solution)/shard_map/all_gather | solution.py:71
  52.4 4.7 %copy-start.1 = (bf16[4,48,6144]{2,1,0:T(8,128)(2,1)S(1)}, bf16[4,48,6144]{2,1,0:T(8,128)(2,1)}, u32[]{:S(2)}) copy-start(bf16[4,48,6144]{2,1,0:T(8,128)(2,1)} %all-gather.4.cloned.1.call-done) | copy-start | bytes 7077892
  136.6 6.9 %copy-start.2 = (s32[4,16]{1,0:T(4,128)S(1)}, s32[4,16]{1,0:T(4,128)}, u32[]{:S(2)}) copy-start(s32[4,16]{1,0:T(4,128)} %param.13) | copy-start | bytes 772
  172.0 16.1 %copy-start = (s32[128]{0:T(128)S(1)}, s32[128]{0:T(128)}, u32[]{:S(2)}) copy-start(s32[128]{0:T(128)} %param.11) | copy-start | bytes 1540
  172.0 16.1 %copy-start.3 = (s32[4]{0:T(128)S(1)}, s32[4]{0:T(128)}, u32[]{:S(2)}) copy-start(s32[4]{0:T(128)} %param.12) | copy-start | bytes 52
  228.0 9.5 %slice-start = ((s8[8388608]{0:T(1024)(128)(4,1)}), s8[4194304]{0:T(1024)(128)(4,1)S(1)}, s32[]{:S(2)}) async-start(s8[8388608]{0:T(1024)(128)(4,1)} %bitcast.45), calls=%async_computation.3 | async-start | bytes 8388608
  228.3 9.2 %slice-start.1 = ((s8[8388608]{0:T(1024)(128)(4,1)}), s8[4194304]{0:T(1024)(128)(4,1)S(1)}, s32[]{:S(2)}) async-start(s8[8388608]{0:T(1024)(128)(4,1)} %bitcast.45), calls=%async_computation.4 | async-start | bytes 8388608
Sparse Core Ops, SparseCore 0:
  9.8 42.5 all-gather.3
  54.9 73.2 all-gather.5
  143.6 71.1 all-gather.7
where the time goes:
time: 251 us; the launch traced here: 250 us
  waiting for transfers between devices  118 us (47%)
  local copies, waits for them, and re-layouts  61 us (24%)
  matrix products  27.4 us (11%)
  between operations  14.7 us (6%)
  blocking collectives  14.5 us (6%)
  other arithmetic  14.1 us (6%)
    all_gather x1, waiting for transfers between devices, per_device(): lax.all_gather(w_qkv, 'req', axis=0, tiled=True)  70.1 us
    all_gather x1, waiting for transfers between devices, per_device(): lax.all_gather(local_packed, 'req', axis=0, tiled=True)  26.5 us
    all_gather x1, waiting for transfers between devices, per_device(): gathered = lax.all_gather(arrivals, 'wgt', axis=2, tiled=True)  20.2 us
    reshape x1, local copies, waits for them, and re-layouts, per_device(): value_pool[page_table].reshape(req_count, span, local_heads, HEAD)  16.1 us
    reshape x1, local copies, waits for them, and re-layouts, per_device(): key_pool[page_table].reshape(req_count, span, local_heads, HEAD)  16 us
    unnamed x1, blocking collectives  14.5 us
    dot_general x1, matrix products, per_device(): jnp.einsum('jr,rcd->jcd', chooser, lax.all_gather(local_packed, 'req', ax...  9.28 us
    dot_general x1, matrix products, per_device(): jnp.einsum('rqhd,rkhd->rhqk', queries, cached_keys, preferred_element_typ...  7.55 us
  transfers between devices with their start and end apart: 3, of which 3 were waited for; matrix products, arithmetic and copies ran while one was open for 23% of the time, Pallas kernels for 0%

commit v1 on v0

v1 whole, which is shorter than its diff:
```python
import functools
import math

import jax
import jax.numpy as jnp
from jax import lax
from jax.experimental import pallas as pl
from jax.experimental.pallas import tpu as pltpu
from jax.sharding import PartitionSpec as P

HEAD = 96
ROT = 24
EPS = 1e-05
CHUNK_PAGES = 4


def rotary(block, positions):
    half_rot = ROT // 2
    inverse = jnp.power(10000.0, -jnp.arange(half_rot, dtype=jnp.float32) * 2.0 / ROT)
    angles = positions[:, :, None] * inverse[None, None, :]
    cosine = jnp.cos(angles)[:, :, None, :]
    sine = jnp.sin(angles)[:, :, None, :]
    first = block[..., :half_rot]
    second = block[..., half_rot:ROT]
    return jnp.concatenate(
        [first * cosine - second * sine, second * cosine + first * sine, block[..., ROT:]], axis=-1
    )


def attention_kernel(
    lengths, table, q_ref, k_ref, v_ref, key_pool, value_pool, out_ref, nk_ref, nv_ref, kbuf, vbuf, sems
):
    req_count, maxp = table.shape
    page, width = kbuf.shape[1], kbuf.shape[2]
    fresh = q_ref.shape[0] // req_count
    heads = width // HEAD
    rows = heads * fresh
    span = CHUNK_PAGES * page
    factor = math.log2(math.e) / math.sqrt(HEAD)

    def chunks_of(r):
        return (lengths[r] + (span - 1)) // span

    def copies(r, p):
        slot = r * maxp + p
        number = table[r, p]
        return (
            pltpu.make_async_copy(key_pool.at[number], kbuf.at[slot], sems.at[0, slot]),
            pltpu.make_async_copy(value_pool.at[number], vbuf.at[slot], sems.at[1, slot]),
        )

    for r in range(req_count):

        @pl.loop(0, chunks_of(r) * CHUNK_PAGES)
        def _(p):
            for copy in copies(r, p):
                copy.start()

    nk_ref[...] = k_ref[...]
    nv_ref[...] = v_ref[...]

    lane_head = lax.broadcasted_iota(jnp.int32, (rows, width), 1) // HEAD
    row_head = lax.broadcasted_iota(jnp.int32, (rows, width), 0) // fresh
    own_head = lane_head == row_head
    row_token = lax.broadcasted_iota(jnp.int32, (rows, fresh), 0) % fresh
    causal = row_token >= lax.broadcasted_iota(jnp.int32, (rows, fresh), 1)
    column = lax.broadcasted_iota(jnp.int32, (rows, span), 1)

    for r in range(req_count):
        mine = pl.ds(r * fresh, fresh)
        query = jnp.concatenate([q_ref[mine, :]] * heads, axis=0)
        query = jnp.where(own_head, query, jnp.zeros_like(query))
        scores = lax.dot_general(
            query, k_ref[mine, :], (((1,), (1,)), ((), ())), preferred_element_type=jnp.float32
        )
        scores = jnp.where(causal, scores, -1e30)
        peak = jnp.max(scores, axis=1, keepdims=True)
        weights = jnp.exp2((scores - peak) * factor)
        total = jnp.sum(weights, axis=1, keepdims=True)
        mixed = jnp.dot(
            weights.astype(jnp.bfloat16), v_ref[mine, :], preferred_element_type=jnp.float32
        )
        length = lengths[r]

        def step(n, carry):
            peak, total, mixed = carry
            for p in range(CHUNK_PAGES):
                for copy in copies(r, n * CHUNK_PAGES + p):
                    copy.wait()
            here = pl.ds(r * maxp + n * CHUNK_PAGES, CHUNK_PAGES)
            keys = kbuf[here].reshape(span, width)
            values = vbuf[here].reshape(span, width)
            scores = lax.dot_general(
                query, keys, (((1,), (1,)), ((), ())), preferred_element_type=jnp.float32
            )
            scores = jnp.where(column < length - n * span, scores, -1e30)
            higher = jnp.maximum(peak, jnp.max(scores, axis=1, keepdims=True))
            shrink = jnp.exp2((peak - higher) * factor)
            weights = jnp.exp2((scores - higher) * factor)
            total = total * shrink + jnp.sum(weights, axis=1, keepdims=True)
            mixed = mixed * shrink + jnp.dot(
                weights.astype(jnp.bfloat16), values, preferred_element_type=jnp.float32
            )
            return higher, total, mixed

        peak, total, mixed = lax.fori_loop(0, chunks_of(r), step, (peak, total, mixed))
        mixed = jnp.where(own_head, mixed / total, 0.0)
        summed = mixed[:fresh]
        for h in range(1, heads):
            summed = summed + mixed[h * fresh : (h + 1) * fresh]
        out_ref[mine, :] = summed.astype(out_ref.dtype)


def attention(lengths, table, q, k, v, key_pool, value_pool):
    rows, width = q.shape
    page = key_pool.shape[1]
    slots = table.shape[0] * table.shape[1]
    out = jax.ShapeDtypeStruct((rows, width), jnp.bfloat16)
    vmem = pl.BlockSpec(memory_space=pltpu.VMEM)
    smem = pl.BlockSpec(memory_space=pltpu.SMEM)
    anywhere = pl.BlockSpec(memory_space=pl.ANY)
    return pl.pallas_call(
        attention_kernel,
        out_shape=(out, out, out),
        in_specs=[smem, smem, vmem, vmem, vmem, anywhere, anywhere],
        out_specs=(vmem, vmem, vmem),
        scratch_shapes=[
            pltpu.VMEM((slots, page, width), jnp.bfloat16),
            pltpu.VMEM((slots, page, width), jnp.bfloat16),
            pltpu.SemaphoreType.DMA((2, slots)),
        ],
        compiler_params=pltpu.CompilerParams(vmem_limit_bytes=40 << 20),
    )(lengths, table, q, k, v, key_pool, value_pool)


def per_device(
    arrivals, group_of, lengths, page_table, ln_gain, ln_bias, w_qkv, qkv_bias, key_pool, value_pool
):
    req_count, fresh, part = arrivals.shape
    model_width = ln_gain.shape[0]
    local_cols = w_qkv.shape[1]
    local_heads = local_cols // (3 * HEAD)
    everyone = group_of.shape[0]
    devices = everyone // req_count
    groups = devices // 2
    half = part // 2
    each = fresh // groups
    order = jnp.argsort(group_of, stable=True).astype(jnp.int32)

    pieces = arrivals.reshape(req_count, each, groups, 2, half).transpose(2, 3, 0, 1, 4)
    pieces = pieces.reshape(devices, req_count, each * half)
    pieces = lax.all_to_all(pieces, "req", 0, 0, tiled=True)
    pieces = pieces.reshape(everyone, each * half)[order].reshape(devices, req_count, each * half)
    pieces = lax.all_to_all(pieces, "req", 0, 0, tiled=True)
    pieces = pieces.reshape(groups, 2, req_count, each, half).transpose(2, 3, 0, 1, 4)
    tokens = pieces.reshape(req_count * fresh, part)

    gathered = lax.all_gather(tokens, "wgt", axis=1, tiled=True)
    widened = gathered.astype(jnp.float32)
    center = jnp.mean(widened, axis=-1, keepdims=True)
    spread = jnp.mean(jnp.square(widened - center), axis=-1, keepdims=True)
    normed = (widened - center) * lax.rsqrt(spread + EPS) * ln_gain.astype(
        jnp.float32
    ) + ln_bias.astype(jnp.float32)
    summed = jnp.dot(
        normed.astype(jnp.bfloat16),
        lax.all_gather(w_qkv, "req", axis=0, tiled=True),
        preferred_element_type=jnp.float32,
    )
    summed = summed + qkv_bias.astype(jnp.float32)
    projected = summed.reshape(req_count, fresh, local_heads, 3, HEAD)
    positions = (
        lengths[:, None] + jnp.arange(fresh, dtype=jnp.int32)[None, :]
    ).astype(jnp.float32)
    flat = (req_count * fresh, local_heads * HEAD)
    q = rotary(projected[:, :, :, 0], positions).astype(jnp.bfloat16).reshape(flat)
    k = rotary(projected[:, :, :, 1], positions).astype(jnp.bfloat16).reshape(flat)
    v = projected[:, :, :, 2].astype(jnp.bfloat16).reshape(flat)
    outs = attention(lengths, page_table, q, k, v, key_pool, value_pool)
    return tuple(a.reshape(req_count, fresh, local_heads * HEAD) for a in outs)


def solution(mesh):
    in_specs = (
        P("req", None, "wgt"),
        P(),
        P("req"),
        P("req", None),
        P(),
        P(),
        P("req", "wgt"),
        P("wgt"),
        P("req", None, "wgt"),
        P("req", None, "wgt"),
    )
    out_specs = (P("req", None, "wgt"), P("req", None, "wgt"), P("req", None, "wgt"))
    return jax.shard_map(
        per_device, mesh=mesh, in_specs=in_specs, out_specs=out_specs, check_vma=False
    )
```

time: 251 us -> 202 us (0.80)
  local copies, waits for them, and re-layouts: 61 us -> 13 us
  Pallas kernels: 0 us -> 19.9 us
  matrix products: 27.4 us -> 8.38 us
  starting transfers between devices: 0.11 us -> 8.85 us
  other arithmetic: 14.1 us -> 9.91 us
  waiting for transfers between devices: 118 us -> 114 us
    reshape x5 -> x8, local copies, waits for them, and re-layouts: 35.3 us -> 4.04 us  [the longest x1 1.45 us: per_device(): projected = summed.reshape(req_count, fresh, local_heads, 3, HEAD)]
    pallas_call x0 -> x1, Pallas kernels: none -> 19.9 us  [attention(): pl.pallas_call(attention_kernel, out_shape=(out, out, out), in_specs=[sme...]
    dot_general x6 -> x1, matrix products: 27.4 us -> 8.38 us  [per_device(): jnp.dot(normed.astype(jnp.bfloat16), lax.all_gather(w_qkv, 'req', axis=0,...]
    unnamed x1 -> x0, blocking collectives: 14.5 us -> none
    gather x5 -> x1, local copies, waits for them, and re-layouts: 15 us -> 0.9 us  [per_device(): pieces.reshape(everyone, each * half)[order]]
    all_to_all x0 -> x1, blocking collectives: none -> 12.8 us  [per_device(): pieces = lax.all_to_all(pieces, 'req', 0, 0, tiled=True)]
    all_gather x2 -> x1, waiting for transfers between devices: 46.8 us -> 36.4 us  [per_device(): gathered = lax.all_gather(tokens, 'wgt', axis=1, tiled=True)]
    all_to_all x0 -> x1, starting transfers between devices: none -> 8.59 us  [per_device(): pieces = lax.all_to_all(pieces, 'req', 0, 0, tiled=True)]
  transfers between devices with their start and end apart: 3 -> 3, of which waited for: 3 -> 3; matrix products, arithmetic and copies ran while one was open for 23% -> 4% of each run, Pallas kernels for 0% -> 0%
where the time goes in v1:
time: 202 us
  waiting for transfers between devices  114 us (56%)
  Pallas kernels  19.9 us (10%)
  between operations  14.3 us (7%)
  local copies, waits for them, and re-layouts  13 us (6%)
  blocking collectives  12.8 us (6%)
  other arithmetic  9.91 us (5%)
  starting transfers between devices  8.85 us (4%)
  matrix products  8.38 us (4%)
    all_gather x1, waiting for transfers between devices, per_device(): lax.all_gather(w_qkv, 'req', axis=0, tiled=True)  71.5 us
    all_gather x1, waiting for transfers between devices, per_device(): gathered = lax.all_gather(tokens, 'wgt', axis=1, tiled=True)  36.4 us
    pallas_call x1, Pallas kernels, attention(): pl.pallas_call(attention_kernel, out_shape=(out, out, out), in_specs=[sme...  19.9 us
    all_to_all x1, blocking collectives, per_device(): pieces = lax.all_to_all(pieces, 'req', 0, 0, tiled=True)  12.8 us
    all_to_all x1, starting transfers between devices, per_device(): pieces = lax.all_to_all(pieces, 'req', 0, 0, tiled=True)  8.59 us
    dot_general x1, matrix products, per_device(): jnp.dot(normed.astype(jnp.bfloat16), lax.all_gather(w_qkv, 'req', axis=0,...  8.38 us
    all_to_all x1, waiting for transfers between devices, per_device(): pieces = lax.all_to_all(pieces, 'req', 0, 0, tiled=True)  5.96 us
    unnamed x17, local copies, waits for them, and re-layouts  5.03 us
  transfers between devices with their start and end apart: 3, of which 3 were waited for; matrix products, arithmetic and copies ran while one was open for 4% of the time, Pallas kernels for 0%

profile of v1, /device:TPU:1, one launch (start us, length us, event | category | flops | bytes accessed | tf_op | source)
XLA Modules:
  0.0 201.5 jit_solution(9083556656652551657)
XLA Ops:
  7.2 1.0 reshape.91
  8.2 0.2 copy.35
  8.4 0.0 copy-start.5
  8.4 0.0 copy-start.6
  8.4 0.0 copy-start.7
  8.4 0.0 copy-start.3
  8.5 0.3 reshape.92
  8.7 0.9 copy.28
  9.6 8.6 %all-to-all-start = ((bf16[32,4,1152]{2,1,0:T(4,128)(2,1)}), bf16[32,4,1152]{2,1,0:T(4,128)(2,1)S(1)}, u32[]{:S(2)}, u32[]{:S(2)}) async-start(bf16[32,4,1152]{2,1,0:T(4,128)(2,1)} %copy.28), calls=%async_computation | async-start | bytes 589824 | tf_op jit(solution)/shard_map/all_to_all | solution.py:152
  18.2 0.0 all-gather.3.cloned.1.call-start
  18.2 3.2 %sort.17 = (s32[128]{0:T(128)}, s32[128]{0:T(128)S(1)}) sort(s32[128]{0:T(128)} %param.11, s32[128]{0:T(128)S(1)} %iota.17), dimensions={0}, to_apply=%region_0.0 | sort | flops 896 | bytes 2048 | tf_op jit(solution)/shard_map/jit(argsort)/sort | solution.py:148
  21.4 6.0 %all-to-all-done = bf16[32,4,1152]{2,1,0:T(4,128)(2,1)S(1)} async-done(((bf16[32,4,1152]{2,1,0:T(4,128)(2,1)}), bf16[32,4,1152]{2,1,0:T(4,128)(2,1)S(1)}, u32[]{:S(2)}, u32[]{:S(2)}) %all-to-all-start) | async-done | bytes 294944 | tf_op jit(solution)/shard_map/all_to_all | solution.py:152
  27.4 0.1 reshape.93
  27.5 0.9 gather_fusion
  28.4 0.1 reshape.94
  28.5 12.8 %all_to_all.10 = bf16[32,4,1152]{2,1,0:T(4,128)(2,1)S(1)} all-to-all(bf16[32,4,1152]{2,1,0:T(4,128)(2,1)S(1)} %reshape.94), channel_id=1, replica_groups=mesh['req'=32,'wgt'=8] {'req'}, dimensions={0} | all-to-all | bytes 589824 | tf_op jit(solution)/shard_map/all_to_all | solution.py:154
  41.3 0.1 reshape.95
  41.4 0.3 copy.30
  41.6 0.8 copy.33
  42.4 0.0 all-gather.3.cloned.1.call-update
  42.4 0.2 all-gather.5.cloned.1.call-start
  42.6 0.5 all-gather.5.cloned.1.call-update
  43.2 0.0 copy-done.5
  43.2 0.0 copy-done.6
  43.2 0.0 copy-done.7
  43.2 0.0 copy-done.3
  43.3 0.1 add_convert_fusion.2
  43.3 0.4 multiply_cosine_fusion
  43.8 36.4 %all-gather.3.cloned.1.call-done = bf16[192,6144]{1,0:T(8,128)(2,1)} async-done(((bf16[192,768]{1,0:T(8,128)(2,1)}), bf16[192,6144]{1,0:T(8,128)(2,1)}) %all-gather.3.cloned.1.call-update) | async-done | bytes 2359312 | tf_op jit(solution)/shard_map/all_gather | solution.py:158
  80.2 0.0 copy-start.4
  80.2 2.2 %convert_reduce_fusion = f32[192]{0:T(256)S(1)} fusion(bf16[192,6144]{1,0:T(8,128)(2,1)} %all-gather.3.cloned.1.call-done), kind=kLoop, calls=%fused_computation.2 | loop fusion | flops 2359104 | bytes 2360064 | tf_op jit(solution)/shard_map/reduce_sum | solution.py:160
  82.4 2.4 %fusion.2 = f32[192]{0:T(256)S(1)} fusion(bf16[192,6144]{1,0:T(8,128)(2,1)} %all-gather.3.cloned.1.call-done, f32[192]{0:T(256)S(1)} %broadcast_multiply_fusion), kind=kLoop, calls=%fused_computation.5 | loop fusion | flops 4718400 | bytes 2360832 | tf_op jit(solution)/shard_map/reduce_sum | solution.py:161
  84.8 71.5 %all-gather.5.cloned.1.call-done = bf16[6144,1152]{1,0:T(8,128)(2,1)} async-done(((bf16[192,1152]{1,0:T(8,128)(2,1)}), bf16[6144,1152]{1,0:T(8,128)(2,1)}) %all-gather.5.cloned.1.call-update) | async-done | bytes 14155792 | tf_op jit(solution)/shard_map/all_gather | solution.py:167
  156.4 0.0 copy-done.4
  156.4 8.4 %convolution_add_fusion = f32[192,1152]{1,0:T(8,128)S(1)} fusion(bf16[6144,1152]{1,0:T(8,128)(2,1)} %all-gather.5.cloned.1.call-done, bf16[192,6144]{1,0:T(8,128)(2,1)S(1)} %copy-done.4, f32[6144]{0:T(1024)S(1)} %convert_element_type.39, f32[6144]{0:T(1024)S(1)} %convert_element_type.38, f32[192]{0:T(256)S(1)} %add_rsqrt_fusion, ...), kind=kOutput, calls=%fused_computation.9 | convolution fusion | flops 2725208064 | bytes 17455104 | tf_op jit(solution)/shard_map/dot_general | solution.py:165
  164.8 0.0 copy-start.2
  164.8 1.5 reshape.97
  166.2 0.6 fusion.12
  166.9 1.3 fusion.11
  168.2 0.2 slice.63
  168.3 0.2 slice.64
  168.5 0.7 subtract_convert_fusion
  169.2 0.9 pad_maximum_fusion
  170.0 0.2 convert_element_type.43.q_ref
  170.2 0.2 convert_element_type.44.k_ref
  170.4 0.2 convert_element_type.45.v_ref
  170.6 0.0 copy-done.2
  170.6 0.0 copy-start
  170.6 2.1 %copy-done = bf16[40,128,384]{2,1,0:T(8,128)(2,1)S(1)} copy-done((bf16[40,128,384]{2,1,0:T(8,128)(2,1)S(1)}, bf16[40,128,384]{2,1,0:T(8,128)(2,1)}, u32[]{:S(2)}) %copy-start) | copy-done | bytes 3932184
  172.7 0.0 copy-start.1
  172.7 2.1 %copy-done.1 = bf16[40,128,384]{2,1,0:T(8,128)(2,1)S(1)} copy-done((bf16[40,128,384]{2,1,0:T(8,128)(2,1)S(1)}, bf16[40,128,384]{2,1,0:T(8,128)(2,1)}, u32[]{:S(2)}) %copy-start.1) | copy-done | bytes 3932184
  174.8 19.9 %shard_map.121 = (bf16[192,384]{1,0:T(8,128)(2,1)}, bf16[192,384]{1,0:T(8,128)(2,1)}, bf16[192,384]{1,0:T(8,128)(2,1)}) custom-call(s32[4]{0:T(128)S(1)} %copy-done.3, s32[4,16]{1,0:T(4,128)S(1)} %copy-done.2, bf16[192,384]{1,0:T(8,128)(2,1)S(1)} %convert_element_type.43.q_ref, bf16[192,384]{1,0:T(8,128)(2,1)S(1)} %convert_element_type.44.k_ref, ...), custom_call_target="tpu_custom_call" | custom-call | tf_op jit(solution)/shard_map/pallas_call | solution.py:122
  (10 shorter events, 0.1 us)
Async XLA Ops:
  8.4 34.8 %copy-start.5 = (bf16[6144]{0:T(1024)(128)(2,1)S(1)}, bf16[6144]{0:T(1024)(128)(2,1)}, u32[]{:S(2)}) copy-start(bf16[6144]{0:T(1024)(128)(2,1)} %param.14) | copy-start | bytes 36868
  8.4 34.8 %copy-start.6 = (bf16[6144]{0:T(1024)(128)(2,1)S(1)}, bf16[6144]{0:T(1024)(128)(2,1)}, u32[]{:S(2)}) copy-start(bf16[6144]{0:T(1024)(128)(2,1)} %param.15) | copy-start | bytes 36868
  8.4 34.8 %copy-start.7 = (bf16[1152]{0:T(1024)(128)(2,1)S(1)}, bf16[1152]{0:T(1024)(128)(2,1)}, u32[]{:S(2)}) copy-start(bf16[1152]{0:T(1024)(128)(2,1)} %param.17) | copy-start | bytes 6916
  8.4 34.8 %copy-start.3 = (s32[4]{0:T(128)S(1)}, s32[4]{0:T(128)}, u32[]{:S(2)}) copy-start(s32[4]{0:T(128)} %lengths.1) | copy-start | bytes 52
  9.6 17.8 %all-to-all-start = ((bf16[32,4,1152]{2,1,0:T(4,128)(2,1)}), bf16[32,4,1152]{2,1,0:T(4,128)(2,1)S(1)}, u32[]{:S(2)}, u32[]{:S(2)}) async-start(bf16[32,4,1152]{2,1,0:T(4,128)(2,1)} %copy.28), calls=%async_computation | async-start | bytes 589824 | tf_op jit(solution)/shard_map/all_to_all | solution.py:152
  18.2 62.0 %all-gather.3.cloned.1.call-start = ((), (), s32[]{:S(2)}) async-start(), calls=%async_computation.2 | async-start | bytes 2654208 | tf_op jit(solution)/shard_map/all_gather | solution.py:158
  42.4 114.0 %all-gather.5.cloned.1.call-start = ((), (), s32[]{:S(2)}) async-start(), calls=%async_computation.3 | async-start | bytes 14598144 | tf_op jit(solution)/shard_map/all_gather | solution.py:167
  80.2 76.2 %copy-start.4 = (bf16[192,6144]{1,0:T(8,128)(2,1)S(1)}, bf16[192,6144]{1,0:T(8,128)(2,1)}, u32[]{:S(2)}) copy-start(bf16[192,6144]{1,0:T(8,128)(2,1)} %all-gather.3.cloned.1.call-done) | copy-start | bytes 7077892
  164.8 5.8 %copy-start.2 = (s32[4,16]{1,0:T(4,128)S(1)}, s32[4,16]{1,0:T(4,128)}, u32[]{:S(2)}) copy-start(s32[4,16]{1,0:T(4,128)} %table.1) | copy-start | bytes 772
  170.6 2.1 %copy-start = (bf16[40,128,384]{2,1,0:T(8,128)(2,1)S(1)}, bf16[40,128,384]{2,1,0:T(8,128)(2,1)}, u32[]{:S(2)}) copy-start(bf16[40,128,384]{2,1,0:T(8,128)(2,1)} %key_pool.1) | copy-start | bytes 11796484
  172.7 2.1 %copy-start.1 = (bf16[40,128,384]{2,1,0:T(8,128)(2,1)S(1)}, bf16[40,128,384]{2,1,0:T(8,128)(2,1)}, u32[]{:S(2)}) copy-start(bf16[40,128,384]{2,1,0:T(8,128)(2,1)} %value_pool.1) | copy-start | bytes 11796484
Sparse Core Ops, SparseCore 0:
  42.5 37.5 all-gather.2
  82.7 73.6 all-gather.4

commit v2 on v1

--- a/solution.py
+++ b/solution.py
@@ -1,4 +1,3 @@
-import functools
 import math
 
 import jax
@@ -7,24 +6,12 @@
 from jax.experimental import pallas as pl
 from jax.experimental.pallas import tpu as pltpu
 from jax.sharding import PartitionSpec as P
+import numpy as np
 
 HEAD = 96
 ROT = 24
 EPS = 1e-05
 CHUNK_PAGES = 4
-
-
-def rotary(block, positions):
-    half_rot = ROT // 2
-    inverse = jnp.power(10000.0, -jnp.arange(half_rot, dtype=jnp.float32) * 2.0 / ROT)
-    angles = positions[:, :, None] * inverse[None, None, :]
-    cosine = jnp.cos(angles)[:, :, None, :]
-    sine = jnp.sin(angles)[:, :, None, :]
-    first = block[..., :half_rot]
-    second = block[..., half_rot:ROT]
-    return jnp.concatenate(
-        [first * cosine - second * sine, second * cosine + first * sine, block[..., ROT:]], axis=-1
-    )
 
 
 def attention_kernel(
@@ -118,7 +105,7 @@
     out = jax.ShapeDtypeStruct((rows, width), jnp.bfloat16)
     vmem = pl.BlockSpec(memory_space=pltpu.VMEM)
     smem = pl.BlockSpec(memory_space=pltpu.SMEM)
-    anywhere = pl.BlockSpec(memory_space=pl.ANY)
+    anywhere = pl.BlockSpec(memory_space=pltpu.HBM)
     return pl.pallas_call(
         attention_kernel,
         out_shape=(out, out, out),
@@ -133,51 +120,422 @@
     )(lengths, table, q, k, v, key_pool, value_pool)
 
 
+MESH = pl.DeviceIdType.MESH
+SIDE = 4
+CHIPS = SIDE * SIDE
+DEPTH = 8
+OFFSETS = (0, -1, 1, 2)
+
+
+def copy_numbers():
+    names = []
+    for h in (0, 1):
+        names += [("own", h, s) for s in (1, -1)]
+        names += [("own on", h, s) for s in (1, -1)]
+        names += [("row", h, du, s) for du in OFFSETS for s in (1, -1)]
+        names += [("row on", h, du, s) for du in OFFSETS for s in (1, -1)]
+        names += [("core", h, du, dv) for du in OFFSETS for dv in OFFSETS]
+    names += [("z", k, s) for k in (1, 2, 3, 4) for s in (1, -1)]
+    names.append(("swap",))
+    return {name: number for number, name in enumerate(names)}
+
+
+NUMBER = copy_numbers()
+
+
+def project_kernel(
+    lengths, x_ref, w_ref, group_ref, gain_ref, bias_ref, col_bias_ref, q_ref, k_ref, v_ref,
+    weights, slabs, normed, acc, cosines, sines, means, squares, out1, in1, swapped, out2, in2,
+    send, recv, send1, recv1, send2, recv2,
+):
+    f32, bf16, i32 = jnp.float32, jnp.bfloat16, jnp.int32
+    tokens, part = x_ref.shape
+    depth, cols = w_ref.shape
+    req_count = lengths.shape[0]
+    fresh = tokens // req_count
+    half = part // 2
+    each = fresh // CHIPS
+    width = cols // 3
+    rows_half, rows_sub = depth // 2, depth // 4
+    me, z = lax.axis_index("req"), lax.axis_index("wgt")
+    core = me % 2
+    chip = me // 2
+    y, x = chip // SIDE, chip % SIDE
+    iota = lambda shape, axis: lax.broadcasted_iota(i32, shape, axis)
+
+    def device(number, c=core):
+        return (number * 2 + c, z)
+
+    partner = device(chip, 1 - core)
+
+    barrier = pltpu.get_barrier_semaphore()
+
+    @pl.loop(1, CHIPS)
+    def _(d):
+        pl.semaphore_signal(barrier, 1, device_id=device((chip + d) % CHIPS), device_id_type=MESH)
+
+    pl.semaphore_signal(barrier, 1, device_id=partner, device_id_type=MESH)
+    for s in (1, DEPTH - 1):
+        pl.semaphore_signal(barrier, 1, device_id=(me, (z + s) % DEPTH), device_id_type=MESH)
+
+    def by_kind(value):
+        heads = range(width // HEAD)
+        return jnp.concatenate(
+            [
+                value[:, (h * 3 + kind) * HEAD : (h * 3 + kind + 1) * HEAD]
+                for kind in range(3)
+                for h in heads
+            ],
+            axis=1,
+        )
+
+    def place(number, c):
+        return number // 2, (number % 2) * (2 * depth) + c * depth
+
+    own_pair, own_row = place(chip, core)
+    weights[own_pair, pl.ds(pl.multiple_of(own_row, 64), depth), :] = by_kind(w_ref[...])
+
+    m, n = iota((CHIPS * 8, tokens), 0), iota((CHIPS * 8, tokens), 1)
+    for t in range(each):
+        take = (m % 8) // 2 * fresh + t * CHIPS + m // 8 == n
+        piece = jnp.zeros((CHIPS * 8, half), f32)
+        for h in (0, 1):
+            chosen = jnp.where(take & (m % 2 == h), 1.0, 0.0).astype(bf16)
+            piece += jnp.dot(chosen, x_ref[:, h * half : (h + 1) * half], preferred_element_type=f32)
+        out1[:, :, t * half : (t + 1) * half] = piece.reshape(CHIPS, 8, half).astype(bf16)
+    in1[chip] = out1[chip]
+
+    pl.semaphore_wait(barrier, CHIPS - 1 + 3)
+
+    def spread(source, target, send_sems, recv_sems):
+        def copy(d):
+            other = (chip + d) % CHIPS
+            return pltpu.make_async_remote_copy(
+                src_ref=source.at[other],
+                dst_ref=target.at[chip],
+                send_sem=send_sems.at[d],
+                recv_sem=recv_sems.at[d],
+                device_id=device(other),
+                device_id_type=MESH,
+            )
+
+        return copy
+
+    first, second = spread(out1, in1, send1, recv1), spread(out2, in2, send2, recv2)
+
+    @pl.loop(1, CHIPS)
+    def _(d):
+        first(d).start()
+
+    def remote(name, ref, target, dst=None):
+        return pltpu.make_async_remote_copy(
+            src_ref=ref,
+            dst_ref=ref if dst is None else dst,
+            send_sem=send.at[NUMBER[name]],
+            recv_sem=recv.at[NUMBER[name]],
+            device_id=target,
+            device_id_type=MESH,
+        )
+
+    where = {0: (x, y), 1: (y, x)}
+
+    def chip_at(h, du, dv):
+        u, v = where[h]
+        u, v = (u + du + SIDE) % SIDE, (v + dv + SIDE) % SIDE
+        return v * SIDE + u if h == 0 else u * SIDE + v
+
+    def block(h, du, dv, c=core, sub=None):
+        pair, row = place(chip_at(h, du, dv), c)
+        row = row + h * rows_half + (0 if sub in (None, 1) else rows_sub)
+        return weights.at[pair, pl.ds(pl.multiple_of(row, 16), rows_half if sub is None else rows_sub), :]
+
+    def weight_copy(name):
+        kind, h = name[0], name[1]
+        if kind == "own":
+            return remote(name, block(h, 0, 0), device(chip_at(h, name[2], 0)))
+        if kind == "own on":
+            s = name[2]
+            return remote(name, block(h, -s, 0, sub=s), device(chip_at(h, s, 0)))
+        if kind == "row":
+            du, s = name[2], name[3]
+            return remote(name, block(h, du, 0), device(chip_at(h, 0, s)))
+        if kind == "row on":
+            du, s = name[2], name[3]
+            return remote(name, block(h, du, -s, sub=s), device(chip_at(h, 0, s)))
+        du, dv = name[2], name[3]
+        return remote(name, block(h, du, dv), partner)
+
+    started = []
+
+    def start(*name):
+        weight_copy(name).start()
+        started.append(name)
+
+    def arrive(*name):
+        weight_copy(name).wait_recv()
+
+    for h in (0, 1):
+        for s in (1, -1):
+            start("own", h, s)
+    for h in (0, 1):
+        start("core", h, 0, 0)
+
+    a, b = iota((CHIPS * 8, CHIPS * 8), 0), iota((CHIPS * 8, CHIPS * 8), 1)
+    group_row = jnp.broadcast_to(group_ref[...], a.shape)
+    group_col = jnp.sum(jnp.where(a == b, group_row, 0), axis=1, keepdims=True)
+    rank = jnp.sum(jnp.where((group_col == group_row) & (a < b), 1, 0), axis=0, keepdims=True)
+    slot_row = group_ref[...] * req_count + rank
+    slot_col = jnp.sum(jnp.where(a == b, jnp.broadcast_to(slot_row, a.shape), 0), axis=1, keepdims=True)
+
+    def selector(c):
+        arriving = (b // 8 * 2 + c) * req_count + b % 8 // 2
+        slot = jnp.sum(jnp.where(a == arriving, slot_col, 0), axis=0, keepdims=True)
+        wanted = (a // 8 * 2 + core) * req_count + a % 8 // 2
+        return jnp.where((wanted == slot) & (a % 2 == b % 2), 1.0, 0.0).astype(bf16)
+
+    pick_own, pick_other = selector(core), selector(1 - core)
+
+    @pl.loop(1, CHIPS)
+    def _(d):
+        first(d).wait_recv()
+
+    swap = remote(("swap",), in1, partner, swapped)
+    swap.start()
+
+    def flat(ref):
+        return ref[...].astype(f32).reshape(CHIPS * 8, each * half).astype(bf16)
+
+    mixed = jnp.dot(pick_own, flat(in1), preferred_element_type=f32)
+    swap.wait_recv()
+    mixed = mixed + jnp.dot(pick_other, flat(swapped), preferred_element_type=f32)
+    out2[...] = mixed.reshape(CHIPS, 8, each * half).astype(bf16)
+    in2[chip] = out2[chip]
+
+    @pl.loop(1, CHIPS)
+    def _(d):
+        second(d).start()
+
+    for h in (0, 1):
+        for s in (1, -1):
+            start("row", h, 0, s)
+
+    lane = iota((1, width), 1) % HEAD
+    inverse = jnp.zeros((1, width), f32)
+    for i in range(ROT // 2):
+        value = float(np.float32(10000.0) ** np.float32(-2.0 * i / ROT))
+        inverse = jnp.where((lane == i) | (lane == i + ROT // 2), value, inverse)
+    for r in range(req_count):
+        mine = pl.ds(r * fresh, fresh)
+        position = (iota((fresh, 1), 0) + lengths[r]).astype(f32)
+        angle = position * inverse
+        cosines[mine, :] = jnp.cos(angle)
+        sines[mine, :] = jnp.where(lane < ROT // 2, -jnp.sin(angle), jnp.sin(angle))
+
+    for h in (0, 1):
+        for s in (1, -1):
+            arrive("own", h, s)
+            start("own on", h, s)
+            start("row", h, -s, 1)
+            start("row", h, -s, -1)
+            start("core", h, -s, 0)
+
+    @pl.loop(1, CHIPS)
+    def _(d):
+        second(d).wait_recv()
+
+    m, n = iota((req_count * CHIPS, CHIPS * 8), 0), iota((req_count * CHIPS, CHIPS * 8), 1)
+    pieces = flat(in2)
+    for h in (0, 1):
+        chosen = jnp.where(m % CHIPS * 8 + m // CHIPS * 2 + h == n, 1.0, 0.0).astype(bf16)
+        for t in range(each):
+            rows = jnp.dot(chosen, pieces[:, t * half : (t + 1) * half], preferred_element_type=f32)
+            for r in range(req_count):
+                slabs[z, pl.ds(r * fresh + t * CHIPS, CHIPS), h * half : (h + 1) * half] = rows[
+                    r * CHIPS : (r + 1) * CHIPS
+                ].astype(bf16)
+
+    def slab(k, s):
+        ref = slabs.at[(z - k * s + DEPTH) % DEPTH]
+        if k < 4:
+            return ref
+        return ref.at[pl.ds(0 if s == 1 else tokens // 2, tokens // 2), :]
+
+    def z_copy(k, s):
+        ref = slab(k - 1, s)
+        if k == 4:
+            ref = ref.at[pl.ds(0 if s == 1 else tokens // 2, tokens // 2), :]
+        return remote(("z", k, s), ref, (me, (z + s + DEPTH) % DEPTH))
+
+    block_rows = 32
+
+    def gather_stats(number):
+        @pl.loop(0, tokens, step=block_rows)
+        def _(row):
+            mine = pl.ds(pl.multiple_of(row, block_rows), block_rows)
+            value = slabs[number, mine, :].astype(f32)
+            mean = jnp.sum(value, axis=1, keepdims=True) * (1.0 / part)
+            rest = value - mean
+            means[number, mine, :] = mean
+            squares[number, mine, :] = jnp.sum(rest * rest, axis=1, keepdims=True)
+
+    def z_step(k):
+        for s in (1, -1):
+            z_copy(k, s).wait_recv()
+            if k < 4:
+                z_copy(k + 1, s).start()
+        if k < 4:
+            gather_stats((z - k + DEPTH) % DEPTH)
+            gather_stats((z + k) % DEPTH)
+        else:
+            gather_stats((z + k) % DEPTH)
+
+    def rows_step(du):
+        for h in (0, 1):
+            for s in (1, -1):
+                arrive("row", h, du, s)
+                start("row on", h, du, s)
+                start("core", h, du, -s)
+
+    for s in (1, -1):
+        z_copy(1, s).start()
+    gather_stats(z)
+
+    for h in (0, 1):
+        for s in (1, -1):
+            arrive("own on", h, s)
+        start("row", h, 2, 1)
+        start("row", h, 2, -1)
+        start("core", h, 2, 0)
+
+    rows_step(0)
+    z_step(1)
+    rows_step(-1)
+    z_step(2)
+    rows_step(1)
+    z_step(3)
+    rows_step(2)
+    z_step(4)
+
+    @pl.loop(0, tokens, step=block_rows)
+    def _(row):
+        mine = pl.ds(pl.multiple_of(row, block_rows), block_rows)
+        mean = means[0, mine, :]
+        for w in range(1, DEPTH):
+            mean = mean + means[w, mine, :]
+        mean = mean * (1.0 / DEPTH)
+        spread_sum = jnp.zeros_like(mean)
+        for w in range(DEPTH):
+            apart = means[w, mine, :] - mean
+            spread_sum = spread_sum + (squares[w, mine, :] + part * (apart * apart))
+        inv = lax.rsqrt(spread_sum * (1.0 / (part * DEPTH)) + EPS)
+        for w in range(DEPTH):
+            here = slice(w * part, (w + 1) * part)
+            value = (slabs[w, mine, :].astype(f32) - mean) * inv
+            value = value * gain_ref[:, here].astype(f32) + bias_ref[:, here].astype(f32)
+            normed[w, mine, :] = value.astype(bf16)
+
+    acc[...] = jnp.broadcast_to(by_kind(col_bias_ref[...].astype(f32)), acc.shape)
+
+    def far(h, du):
+        for s in (1, -1):
+            arrive("row on", h, du, s)
+        start("core", h, du, 2)
+
+    def from_core(h, du, dv):
+        remote(("core", h, du, dv), block(h, du, dv, c=1 - core), partner).wait_recv()
+
+    for dy in OFFSETS:
+        far(1, dy)
+        if dy == 2:
+            for dx in OFFSETS:
+                far(0, dx)
+        for dx in OFFSETS:
+            from_core(0, dx, dy)
+            from_core(1, dy, dx)
+        first_pair = (y + dy + SIDE) % SIDE * 2
+
+        @pl.loop(first_pair, first_pair + 2)
+        def _(pair):
+            acc[...] += jnp.dot(normed[pair], weights[pair], preferred_element_type=f32)
+
+    def turn(value):
+        near = jnp.where(lane < ROT // 2, pltpu.roll(value, width - ROT // 2, 1), pltpu.roll(value, ROT // 2, 1))
+        return value * cosines[...] + near * sines[...]
+
+    q_ref[...] = turn(acc[:, :width]).astype(bf16)
+    k_ref[...] = turn(acc[:, width : 2 * width]).astype(bf16)
+    v_ref[...] = acc[:, 2 * width :].astype(bf16)
+
+    for name in started:
+        weight_copy(name).wait_send()
+    for k in (1, 2, 3, 4):
+        for s in (1, -1):
+            z_copy(k, s).wait_send()
+    swap.wait_send()
+
+    @pl.loop(1, CHIPS)
+    def _(d):
+        first(d).wait_send()
+        second(d).wait_send()
+
+
+def project(lengths, x, w, group_of, gain, bias, col_bias):
+    tokens, part = x.shape
+    depth, cols = w.shape
+    width = cols // 3
+    lanes = tokens * part // (CHIPS * 8)
+    out = jax.ShapeDtypeStruct((tokens, width), jnp.bfloat16)
+    vmem = pl.BlockSpec(memory_space=pltpu.VMEM)
+    message = pltpu.VMEM((CHIPS, 8, lanes), jnp.bfloat16)
+    pairs = pltpu.SemaphoreType.DMA((CHIPS,))
+    copies = pltpu.SemaphoreType.DMA((len(NUMBER),))
+    return pl.pallas_call(
+        project_kernel,
+        out_shape=(out, out, out),
+        in_specs=[pl.BlockSpec(memory_space=pltpu.SMEM)] + [vmem] * 6,
+        out_specs=(vmem, vmem, vmem),
+        scratch_shapes=[
+            pltpu.VMEM((CHIPS // 2, 4 * depth, cols), jnp.bfloat16),
+            pltpu.VMEM((DEPTH, tokens, part), jnp.bfloat16),
+            pltpu.VMEM((DEPTH, tokens, part), jnp.bfloat16),
+            pltpu.VMEM((tokens, cols), jnp.float32),
+            pltpu.VMEM((tokens, width), jnp.float32),
+            pltpu.VMEM((tokens, width), jnp.float32),
+            pltpu.VMEM((DEPTH, tokens, 1), jnp.float32),
+            pltpu.VMEM((DEPTH, tokens, 1), jnp.float32),
+            message,
+            message,
+            message,
+            message,
+            message,
+            copies,
+            copies,
+            pairs,
+            pairs,
+            pairs,
+            pairs,
+        ],
+        compiler_params=pltpu.CompilerParams(
+            collective_id=0, has_side_effects=True, vmem_limit_bytes=48 << 20
+        ),
+    )(lengths, x, w, group_of, gain, bias, col_bias)
+
+
 def per_device(
     arrivals, group_of, lengths, page_table, ln_gain, ln_bias, w_qkv, qkv_bias, key_pool, value_pool
 ):
     req_count, fresh, part = arrivals.shape
-    model_width = ln_gain.shape[0]
-    local_cols = w_qkv.shape[1]
-    local_heads = local_cols // (3 * HEAD)
-    everyone = group_of.shape[0]
-    devices = everyone // req_count
-    groups = devices // 2
-    half = part // 2
-    each = fresh // groups
-    order = jnp.argsort(group_of, stable=True).astype(jnp.int32)
-
-    pieces = arrivals.reshape(req_count, each, groups, 2, half).transpose(2, 3, 0, 1, 4)
-    pieces = pieces.reshape(devices, req_count, each * half)
-    pieces = lax.all_to_all(pieces, "req", 0, 0, tiled=True)
-    pieces = pieces.reshape(everyone, each * half)[order].reshape(devices, req_count, each * half)
-    pieces = lax.all_to_all(pieces, "req", 0, 0, tiled=True)
-    pieces = pieces.reshape(groups, 2, req_count, each, half).transpose(2, 3, 0, 1, 4)
-    tokens = pieces.reshape(req_count * fresh, part)
-
-    gathered = lax.all_gather(tokens, "wgt", axis=1, tiled=True)
-    widened = gathered.astype(jnp.float32)
-    center = jnp.mean(widened, axis=-1, keepdims=True)
-    spread = jnp.mean(jnp.square(widened - center), axis=-1, keepdims=True)
-    normed = (widened - center) * lax.rsqrt(spread + EPS) * ln_gain.astype(
-        jnp.float32
-    ) + ln_bias.astype(jnp.float32)
-    summed = jnp.dot(
-        normed.astype(jnp.bfloat16),
-        lax.all_gather(w_qkv, "req", axis=0, tiled=True),
-        preferred_element_type=jnp.float32,
+    q, k, v = project(
+        lengths,
+        arrivals.reshape(req_count * fresh, part),
+        w_qkv,
+        group_of.reshape(1, -1),
+        ln_gain.reshape(1, -1),
+        ln_bias.reshape(1, -1),
+        qkv_bias.reshape(1, -1),
     )
-    summed = summed + qkv_bias.astype(jnp.float32)
-    projected = summed.reshape(req_count, fresh, local_heads, 3, HEAD)
-    positions = (
-        lengths[:, None] + jnp.arange(fresh, dtype=jnp.int32)[None, :]
-    ).astype(jnp.float32)
-    flat = (req_count * fresh, local_heads * HEAD)
-    q = rotary(projected[:, :, :, 0], positions).astype(jnp.bfloat16).reshape(flat)
-    k = rotary(projected[:, :, :, 1], positions).astype(jnp.bfloat16).reshape(flat)
-    v = projected[:, :, :, 2].astype(jnp.bfloat16).reshape(flat)
     outs = attention(lengths, page_table, q, k, v, key_pool, value_pool)
-    return tuple(a.reshape(req_count, fresh, local_heads * HEAD) for a in outs)
+    return tuple(a.reshape(req_count, fresh, -1) for a in outs)
 
 
 def solution(mesh):

time: 202 us -> 111 us (0.55)
  the two profiles are of different devices: /device:TPU:1 before, /device:TPU:2 now
where the time goes in v2:
time: 111 us; the launch traced here: 110 us
  Pallas kernels  99.4 us (90%)
  local copies, waits for them, and re-layouts  10.3 us (9%)
    pallas_call x1, Pallas kernels, project(): pl.pallas_call(project_kernel, out_shape=(out, out, out), in_specs=[pl.Bl...  77.8 us
    pallas_call x1, Pallas kernels, attention(): pl.pallas_call(attention_kernel, out_shape=(out, out, out), in_specs=[sme...  21.6 us
    unnamed x14, local copies, waits for them, and re-layouts  8.18 us

profile of v2, /device:TPU:2, one launch (start us, length us, event | category | flops | bytes accessed | tf_op | source)
XLA Modules:
  0.0 110.4 jit_solution(15298828877318043731)
XLA Ops:
  0.6 0.7 reshape.34.col_bias_ref
  1.3 0.7 reshape.32.gain_ref
  2.0 0.7 reshape.33.bias_ref
  2.8 0.0 copy-start.2
  2.8 1.0 copy-done.2
  3.8 0.0 copy-start.3
  3.8 1.0 copy-done.3
  4.8 0.0 copy-start.5
  4.8 0.7 copy-done.5
  5.4 0.0 copy-start.6
  5.4 0.7 copy-done.6
  6.1 77.8 %shard_map.121 = (bf16[192,384]{1,0:T(8,128)(2,1)S(1)}, bf16[192,384]{1,0:T(8,128)(2,1)S(1)}, bf16[192,384]{1,0:T(8,128)(2,1)S(1)}) custom-call(s32[4]{0:T(128)S(1)} %copy-done.5, bf16[192,768]{1,0:T(8,128)(2,1)S(1)} %bitcast.5, bf16[192,1152]{1,0:T(8,128)(2,1)S(1)} %copy-done.2, s32[1,128]{1,0:T(1,128)S(1)} %bitcast.6, ...), custom_call_target="tpu_custom_call" | custom-call | tf_op jit(solution)/shard_map/pallas_call | solution.py:492
  83.9 0.0 copy-start
  83.9 2.1 %copy-done = bf16[40,128,384]{2,1,0:T(8,128)(2,1)S(1)} copy-done((bf16[40,128,384]{2,1,0:T(8,128)(2,1)S(1)}, bf16[40,128,384]{2,1,0:T(8,128)(2,1)}, u32[]{:S(2)}) %copy-start) | copy-done | bytes 3932184
  86.0 0.0 copy-start.1
  86.0 2.1 %copy-done.1 = bf16[40,128,384]{2,1,0:T(8,128)(2,1)S(1)} copy-done((bf16[40,128,384]{2,1,0:T(8,128)(2,1)S(1)}, bf16[40,128,384]{2,1,0:T(8,128)(2,1)}, u32[]{:S(2)}) %copy-start.1) | copy-done | bytes 3932184
  88.1 0.0 copy-start.4
  88.1 0.7 copy-done.4
  88.8 21.6 %shard_map.122 = (bf16[192,384]{1,0:T(8,128)(2,1)}, bf16[192,384]{1,0:T(8,128)(2,1)}, bf16[192,384]{1,0:T(8,128)(2,1)}) custom-call(s32[4]{0:T(128)S(1)} %copy-done.5, s32[4,16]{1,0:T(4,128)S(1)} %copy-done.4, bf16[192,384]{1,0:T(8,128)(2,1)S(1)} %get-tuple-element.9.q_ref, bf16[192,384]{1,0:T(8,128)(2,1)S(1)} %get-tuple-element.10.k_ref, ...), custom_call_target="tpu_custom_call" | custom-call | tf_op jit(solution)/shard_map/pallas_call | solution.py:109
Async XLA Ops:
  2.8 1.0 copy-start.2
  3.8 1.0 copy-start.3
  4.8 0.7 copy-start.5
  5.4 0.7 copy-start.6
  83.9 2.1 %copy-start = (bf16[40,128,384]{2,1,0:T(8,128)(2,1)S(1)}, bf16[40,128,384]{2,1,0:T(8,128)(2,1)}, u32[]{:S(2)}) copy-start(bf16[40,128,384]{2,1,0:T(8,128)(2,1)} %key_pool.1) | copy-start | bytes 11796484
  86.0 2.1 %copy-start.1 = (bf16[40,128,384]{2,1,0:T(8,128)(2,1)S(1)}, bf16[40,128,384]{2,1,0:T(8,128)(2,1)}, u32[]{:S(2)}) copy-start(bf16[40,128,384]{2,1,0:T(8,128)(2,1)} %value_pool.1) | copy-start | bytes 11796484
  88.1 0.7 copy-start.4

commit v3 on v2

v3 whole, which is shorter than its diff:
```python
import math

import jax
import jax.numpy as jnp
from jax import lax
from jax.experimental import pallas as pl
from jax.experimental.pallas import tpu as pltpu
from jax.sharding import PartitionSpec as P
import numpy as np

HEAD = 96
ROT = 24
EPS = 1e-05
CHUNK_PAGES = 4
VMEM_BYTES = 67043328


def attention_kernel(
    lengths, table, q_ref, k_ref, v_ref, key_pool, value_pool, out_ref, nk_ref, nv_ref,
    kbuf, vbuf, scores, mixed, sems,
):
    f32, bf16 = jnp.float32, jnp.bfloat16
    req_count, maxp = table.shape
    page, width = kbuf.shape[1], kbuf.shape[2]
    fresh = q_ref.shape[0] // req_count
    heads = width // HEAD
    rows = heads * fresh
    span = CHUNK_PAGES * page
    factor = math.log2(math.e) / math.sqrt(HEAD)
    low = -1e30

    def chunks_of(r):
        return (lengths[r] + (span - 1)) // span

    def key_copy(r, p):
        slot = r * maxp + p
        return pltpu.make_async_copy(key_pool.at[table[r, p]], kbuf.at[slot], sems.at[0, slot])

    def value_copy(r, p):
        slot = r * maxp + p
        return pltpu.make_async_copy(value_pool.at[table[r, p]], vbuf.at[slot], sems.at[1, slot])

    for r in range(req_count):

        @pl.loop(0, chunks_of(r) * CHUNK_PAGES)
        def _(p):
            key_copy(r, p).start()
            value_copy(r, p).start()

    nk_ref[...] = k_ref[...]
    nv_ref[...] = v_ref[...]

    iota = lambda shape, axis: lax.broadcasted_iota(jnp.int32, shape, axis)
    own_head = iota((rows, width), 1) // HEAD == iota((rows, width), 0) // fresh
    causal = iota((rows, fresh), 0) % fresh >= iota((rows, fresh), 1)
    column = iota((1, span), 1)

    def fold(value, op):
        folded = value[:, :128]
        for n in range(1, value.shape[1] // 128):
            folded = op(folded, value[:, n * 128 : (n + 1) * 128])
        return folded

    across = (((1,), (1,)), ((), ()))
    queries, fresh_scores, fresh_peaks = [], [], []
    for r in range(req_count):
        mine = pl.ds(r * fresh, fresh)
        query = jnp.concatenate([q_ref[mine, :]] * heads, axis=0)
        query = jnp.where(own_head, query, jnp.zeros_like(query))
        own = lax.dot_general(query, k_ref[mine, :], across, preferred_element_type=f32)
        own = jnp.where(causal, own, low)
        queries.append(query)
        fresh_scores.append(own)
        fresh_peaks.append(jnp.max(own, axis=1, keepdims=True))

    for r in range(req_count):
        mine = pl.ds(r * fresh, fresh)
        query, length = queries[r], lengths[r]

        def first(n, peak):
            for p in range(CHUNK_PAGES):
                key_copy(r, n * CHUNK_PAGES + p).wait()
            keys = kbuf[pl.ds(r * maxp + n * CHUNK_PAGES, CHUNK_PAGES)].reshape(span, width)
            value = lax.dot_general(query, keys, across, preferred_element_type=f32)
            value = value + jnp.where(column < length - n * span, 0.0, low)
            scores[n] = value
            return jnp.maximum(peak, fold(value, jnp.maximum))

        peak = lax.fori_loop(0, chunks_of(r), first, jnp.full((rows, 128), low, f32))
        peak = jnp.maximum(jnp.max(peak, axis=1, keepdims=True), fresh_peaks[r])
        offset = peak * factor
        weights = jnp.exp2(fresh_scores[r] * factor - offset)
        mixed[...] = jnp.dot(weights.astype(bf16), v_ref[mine, :], preferred_element_type=f32)
        fresh_total = jnp.sum(weights, axis=1, keepdims=True)

        def second(n, total):
            for p in range(CHUNK_PAGES):
                value_copy(r, n * CHUNK_PAGES + p).wait()
            values = vbuf[pl.ds(r * maxp + n * CHUNK_PAGES, CHUNK_PAGES)].reshape(span, width)
            weights = jnp.exp2(scores[n] * factor - offset)
            mixed[...] += jnp.dot(weights.astype(bf16), values, preferred_element_type=f32)
            return total + fold(weights, jnp.add)

        total = lax.fori_loop(0, chunks_of(r), second, jnp.zeros((rows, 128), f32))
        total = jnp.sum(total, axis=1, keepdims=True) + fresh_total
        part = jnp.where(own_head, mixed[...] * (1.0 / total), 0.0)
        summed = part[:fresh]
        for h in range(1, heads):
            summed = summed + part[h * fresh : (h + 1) * fresh]
        out_ref[mine, :] = summed.astype(out_ref.dtype)


def attention(lengths, table, q, k, v, key_pool, value_pool):
    rows, width = q.shape
    page = key_pool.shape[1]
    req_count, maxp = table.shape
    slots = req_count * maxp
    wide = width // HEAD * (rows // req_count)
    out = jax.ShapeDtypeStruct((rows, width), jnp.bfloat16)
    vmem = pl.BlockSpec(memory_space=pltpu.VMEM)
    smem = pl.BlockSpec(memory_space=pltpu.SMEM)
    anywhere = pl.BlockSpec(memory_space=pl.ANY)
    return pl.pallas_call(
        attention_kernel,
        out_shape=(out, out, out),
        in_specs=[smem, smem, vmem, vmem, vmem, anywhere, anywhere],
        out_specs=(vmem, vmem, vmem),
        scratch_shapes=[
            pltpu.VMEM((slots, page, width), jnp.bfloat16),
            pltpu.VMEM((slots, page, width), jnp.bfloat16),
            pltpu.VMEM((maxp // CHUNK_PAGES, wide, CHUNK_PAGES * page), jnp.float32),
            pltpu.VMEM((wide, width), jnp.float32),
            pltpu.SemaphoreType.DMA((2, slots)),
        ],
        compiler_params=pltpu.CompilerParams(vmem_limit_bytes=VMEM_BYTES),
    )(lengths, table, q, k, v, key_pool, value_pool)


MESH = pl.DeviceIdType.MESH
SIDE = 4
CHIPS = SIDE * SIDE
DEPTH = 8
OFFSETS = (0, -1, 1, 2)
THIRDS = 3


def last_parts(s):
    return ((0, None), (1, 0)) if s == 1 else ((2, None), (1, 1))


def copy_numbers():
    names = []
    for h in (0, 1):
        names += [("own", h, s) for s in (1, -1)]
        names += [("own on", h, s) for s in (1, -1)]
        names += [("row", h, du, s) for du in OFFSETS for s in (1, -1)]
        names += [("row on", h, du, s) for du in OFFSETS for s in (1, -1)]
        names += [("core", h, du, dv) for du in OFFSETS for dv in OFFSETS]
    for s in (1, -1):
        names += [("z", k, s, t) for k in (1, 2, 3) for t in range(THIRDS)]
        names += [("z", 4, s, t) for t, _ in last_parts(s)]
    names.append(("swap",))
    return {name: number for number, name in enumerate(names)}


NUMBER = copy_numbers()


def project_kernel(
    lengths, x_hbm, w_hbm, group_ref, gain_ref, bias_ref, col_bias_ref, q_ref, k_ref, v_ref,
    x_ref, w_ref, weights, slabs, normed, acc, cosines, sines, pivot, sums, squares, gains, biases,
    out1, in1, swapped, out2, in2, load, send, recv, send1, recv1, send2, recv2,
):
    f32, bf16, i32 = jnp.float32, jnp.bfloat16, jnp.int32
    tokens, part = x_ref.shape
    depth, cols = w_ref.shape
    model_width = part * DEPTH
    req_count = lengths.shape[0]
    fresh = tokens // req_count
    half = part // 2
    third = tokens // THIRDS
    width = cols // 3
    rows_half, rows_sub = depth // 2, depth // 4
    me, z = lax.axis_index("req"), lax.axis_index("wgt")
    core = me % 2
    chip = me // 2
    y, x = chip // SIDE, chip % SIDE
    iota = lambda shape, axis: lax.broadcasted_iota(i32, shape, axis)

    def device(number, c=core):
        return (number * 2 + c, z)

    partner = device(chip, 1 - core)

    load_x = pltpu.make_async_copy(x_hbm, x_ref, load.at[0])
    load_w = pltpu.make_async_copy(w_hbm, w_ref, load.at[1])
    load_x.start()
    load_w.start()

    barrier = pltpu.get_barrier_semaphore()

    @pl.loop(1, CHIPS)
    def _(d):
        pl.semaphore_signal(barrier, 1, device_id=device((chip + d) % CHIPS), device_id_type=MESH)

    pl.semaphore_signal(barrier, 1, device_id=partner, device_id_type=MESH)
    for s in (1, DEPTH - 1):
        pl.semaphore_signal(barrier, 1, device_id=(me, (z + s) % DEPTH), device_id_type=MESH)

    load_x.wait()
    m, n = iota((CHIPS * 8, tokens), 0), iota((CHIPS * 8, tokens), 1)
    for t in range(THIRDS):
        take = (m % 8) // 2 * fresh + t * CHIPS + m // 8 == n
        piece = jnp.zeros((CHIPS * 8, half), f32)
        for h in (0, 1):
            chosen = jnp.where(take & (m % 2 == h), 1.0, 0.0).astype(bf16)
            piece += jnp.dot(chosen, x_ref[:, h * half : (h + 1) * half], preferred_element_type=f32)
        out1[:, :, t * half : (t + 1) * half] = piece.reshape(CHIPS, 8, half).astype(bf16)
    in1[chip] = out1[chip]

    pl.semaphore_wait(barrier, CHIPS - 1 + 3)

    def spread(source, target, send_sems, recv_sems):
        def copy(d):
            other = (chip + d) % CHIPS
            return pltpu.make_async_remote_copy(
                src_ref=source.at[other],
                dst_ref=target.at[chip],
                send_sem=send_sems.at[d],
                recv_sem=recv_sems.at[d],
                device_id=device(other),
                device_id_type=MESH,
            )

        return copy

    first, second = spread(out1, in1, send1, recv1), spread(out2, in2, send2, recv2)

    @pl.loop(1, CHIPS)
    def _(d):
        first(d).start()

    def by_kind(value):
        heads = range(width // HEAD)
        return jnp.concatenate(
            [
                value[:, (h * 3 + kind) * HEAD : (h * 3 + kind + 1) * HEAD]
                for kind in range(3)
                for h in heads
            ],
            axis=1,
        )

    def place(number, c):
        return number // 2, (number % 2) * (2 * depth) + c * depth

    load_w.wait()
    own_pair, own_row = place(chip, core)
    weights[own_pair, pl.ds(pl.multiple_of(own_row, 64), depth), :] = by_kind(w_ref[...])

    def remote(name, ref, target, dst=None):
        return pltpu.make_async_remote_copy(
            src_ref=ref,
            dst_ref=ref if dst is None else dst,
            send_sem=send.at[NUMBER[name]],
            recv_sem=recv.at[NUMBER[name]],
            device_id=target,
            device_id_type=MESH,
        )

    where = {0: (x, y), 1: (y, x)}

    def chip_at(h, du, dv):
        u, v = where[h]
        u, v = (u + du + SIDE) % SIDE, (v + dv + SIDE) % SIDE
        return v * SIDE + u if h == 0 else u * SIDE + v

    def block(h, du, dv, c=core, sub=None):
        pair, row = place(chip_at(h, du, dv), c)
        row = row + h * rows_half + (0 if sub in (None, 1) else rows_sub)
        return weights.at[pair, pl.ds(pl.multiple_of(row, 16), rows_half if sub is None else rows_sub), :]

    def weight_copy(name):
        kind, h = name[0], name[1]
        if kind == "own":
            return remote(name, block(h, 0, 0), device(chip_at(h, name[2], 0)))
        if kind == "own on":
            s = name[2]
            return remote(name, block(h, -s, 0, sub=s), device(chip_at(h, s, 0)))
        if kind == "row":
            du, s = name[2], name[3]
            return remote(name, block(h, du, 0), device(chip_at(h, 0, s)))
        if kind == "row on":
            du, s = name[2], name[3]
            return remote(name, block(h, du, -s, sub=s), device(chip_at(h, 0, s)))
        du, dv = name[2], name[3]
        return remote(name, block(h, du, dv), partner)

    started = []

    def start(*name):
        weight_copy(name).start()
        started.append(name)

    def arrive(*name):
        weight_copy(name).wait_recv()

    for h in (0, 1):
        for s in (1, -1):
            start("own", h, s)
    for h in (0, 1):
        start("core", h, 0, 0)

    a, b = iota((CHIPS * 8, CHIPS * 8), 0), iota((CHIPS * 8, CHIPS * 8), 1)
    groups = group_ref[...].reshape(1, -1)
    group_row = jnp.broadcast_to(groups, a.shape)
    group_col = jnp.sum(jnp.where(a == b, group_row, 0), axis=1, keepdims=True)
    rank = jnp.sum(jnp.where((group_col == group_row) & (a < b), 1, 0), axis=0, keepdims=True)
    slot_row = groups * req_count + rank
    slot_col = jnp.sum(jnp.where(a == b, jnp.broadcast_to(slot_row, a.shape), 0), axis=1, keepdims=True)

    def selector(c):
        arriving = (b // 8 * 2 + c) * req_count + b % 8 // 2
        slot = jnp.sum(jnp.where(a == arriving, slot_col, 0), axis=0, keepdims=True)
        wanted = (a // 8 * 2 + core) * req_count + a % 8 // 2
        return jnp.where((wanted == slot) & (a % 2 == b % 2), 1.0, 0.0).astype(bf16)

    pick_own, pick_other = selector(core), selector(1 - core)

    @pl.loop(1, CHIPS)
    def _(d):
        first(d).wait_recv()

    swap = remote(("swap",), in1, partner, swapped)
    swap.start()

    def flat(ref):
        return ref[...].astype(f32).reshape(CHIPS * 8, THIRDS * half).astype(bf16)

    mixed = jnp.dot(pick_own, flat(in1), preferred_element_type=f32)
    swap.wait_recv()
    mixed = mixed + jnp.dot(pick_other, flat(swapped), preferred_element_type=f32)
    out2[...] = mixed.reshape(CHIPS, 8, THIRDS * half).astype(bf16)
    in2[chip] = out2[chip]

    @pl.loop(1, CHIPS)
    def _(d):
        second(d).start()

    for h in (0, 1):
        for s in (1, -1):
            start("row", h, 0, s)

    gains[...] = jnp.broadcast_to(gain_ref[...].astype(f32).reshape(1, -1), gains.shape)
    biases[...] = jnp.broadcast_to(bias_ref[...].astype(f32).reshape(1, -1), biases.shape)
    acc[...] = jnp.broadcast_to(by_kind(col_bias_ref[...].astype(f32).reshape(1, -1)), acc.shape)

    lane = iota((1, 128), 1) % 32
    turning = ROT // 2
    inverse = jnp.zeros((1, 128), f32)
    for i in range(turning):
        value = float(np.float32(10000.0) ** np.float32(-2.0 * i / ROT))
        inverse = jnp.where((lane == i) | (lane == i + turning), value, inverse)
    row = iota((tokens, 1), 0)
    request = row % third // CHIPS
    position = row // third * CHIPS + row % CHIPS
    for r in range(req_count):
        position = position + jnp.where(request == r, lengths[r], 0)
    angle = position.astype(f32) * inverse
    cosines[...] = jnp.cos(angle)
    sine = jnp.sin(angle)
    sines[...] = jnp.where(lane < turning, -sine, sine)

    for h in (0, 1):
        for s in (1, -1):
            arrive("own", h, s)
            start("own on", h, s)
            start("row", h, -s, 1)
            start("row", h, -s, -1)
            start("core", h, -s, 0)

    @pl.loop(1, CHIPS)
    def _(d):
        second(d).wait_recv()

    m, n = iota((third, CHIPS * 8), 0), iota((third, CHIPS * 8), 1)
    pieces = flat(in2)
    for h in (0, 1):
        chosen = jnp.where(m % CHIPS * 8 + m // CHIPS * 2 + h == n, 1.0, 0.0).astype(bf16)
        rows = jnp.dot(chosen, pieces, preferred_element_type=f32).astype(bf16)
        for t in range(THIRDS):
            slabs[z, pl.ds(t * third, third), h * half : (h + 1) * half] = rows[:, t * half : (t + 1) * half]

    def slab(k, s, t, piece=None):
        ref = slabs.at[(z - k * s + DEPTH) % DEPTH]
        if piece is None:
            return ref.at[pl.ds(t * third, third), :]
        return ref.at[pl.ds(t * third + piece * (third // 2), third // 2), :]

    def z_copy(k, s, t):
        piece = dict(last_parts(s))[t] if k == 4 else None
        return remote(("z", k, s, t), slab(k - 1, s, t, piece), (me, (z + s + DEPTH) % DEPTH))

    for t in range(THIRDS):
        for s in (1, -1):
            z_copy(1, s, t).start()

    def folded(value):
        total = value[:, :128]
        for j in range(1, part // 128):
            total = total + value[:, j * 128 : (j + 1) * 128]
        return total

    for t in range(THIRDS):
        mine = pl.ds(t * third, third)
        own = jnp.sum(folded(slabs[z, mine, :].astype(f32)), axis=1, keepdims=True) * (1.0 / part)
        pivot[mine, :] = jnp.broadcast_to(own, (third, 128))
    sums[...] = jnp.zeros_like(sums)
    squares[...] = jnp.zeros_like(squares)

    def add_sums(number):
        @pl.loop(0, tokens, step=32)
        def _(start_row):
            mine = pl.ds(pl.multiple_of(start_row, 32), 32)
            origin, total, square = pivot[mine, :], sums[mine, :], squares[mine, :]
            for j in range(part // 128):
                apart = slabs[number, mine, j * 128 : (j + 1) * 128].astype(f32) - origin
                total = total + apart
                square = square + apart * apart
            sums[mine, :] = total
            squares[mine, :] = square

    def z_step(k):
        if k < 4:
            for t in range(THIRDS):
                for s in (1, -1):
                    z_copy(k, s, t).wait_recv()
                    if k < 3 or t in dict(last_parts(s)):
                        z_copy(k + 1, s, t).start()
            add_sums((z - k + DEPTH) % DEPTH)
            add_sums((z + k) % DEPTH)
        else:
            for s in (1, -1):
                for t, _ in last_parts(s):
                    z_copy(4, s, t).wait_recv()
            add_sums((z + 4) % DEPTH)

    def rows_step(du):
        for h in (0, 1):
            for s in (1, -1):
                arrive("row", h, du, s)
                start("row on", h, du, s)
                start("core", h, du, -s)

    for h in (0, 1):
        for s in (1, -1):
            arrive("own on", h, s)
        start("row", h, 2, 1)
        start("row", h, 2, -1)
        start("core", h, 2, 0)

    add_sums(z)
    z_step(1)
    rows_step(0)
    z_step(2)
    rows_step(-1)
    z_step(3)
    rows_step(1)
    z_step(4)

    def normalise(start_row):
        mine = pl.ds(pl.multiple_of(start_row, 32), 32)
        shift = jnp.sum(sums[mine, :], axis=1, keepdims=True) * (1.0 / model_width)
        square = jnp.sum(squares[mine, :], axis=1, keepdims=True) * (1.0 / model_width)
        inv = jnp.broadcast_to(lax.rsqrt(jnp.maximum(square - shift * shift, 0.0) + EPS), (32, 128))
        mean = pivot[mine, :] + shift
        for j in range(model_width // 128):
            w, lanes = j * 128 // part, slice(j * 128 % part, j * 128 % part + 128)
            value = (slabs[w, mine, lanes].astype(f32) - mean) * inv
            value = value.reshape(4, 8, 128) * gains[:, j * 128 : (j + 1) * 128][None]
            value = value + biases[:, j * 128 : (j + 1) * 128][None]
            normed[w, mine, lanes] = value.reshape(32, 128).astype(bf16)

    pl.loop(0, tokens, step=32)(normalise)

    rows_step(2)

    def far(h, du):
        for s in (1, -1):
            arrive("row on", h, du, s)
        start("core", h, du, 2)

    def from_core(h, du, dv):
        remote(("core", h, du, dv), block(h, du, dv, c=1 - core), partner).wait_recv()

    for dy in OFFSETS:
        far(1, dy)
        if dy == 2:
            for dx in OFFSETS:
                far(0, dx)
        for dx in OFFSETS:
            from_core(0, dx, dy)
            from_core(1, dy, dx)
        first_pair = (y + dy + SIDE) % SIDE * 2

        @pl.loop(first_pair, first_pair + 2)
        def _(pair):
            acc[...] += jnp.dot(normed[pair], weights[pair], preferred_element_type=f32)

    def turn(value):
        lanes = iota((1, width), 1) % HEAD
        forward, backward = pltpu.roll(value, width - turning, 1), pltpu.roll(value, turning, 1)
        near = jnp.where(lanes < turning, forward, backward)
        cosine = jnp.concatenate([cosines[...]] * (width // 128), axis=1)
        sine = jnp.concatenate([sines[...]] * (width // 128), axis=1)
        return jnp.where(lanes < ROT, value * cosine + near * sine, value)

    def put(ref, value):
        value = value.astype(bf16)
        for t in range(THIRDS):
            for r in range(req_count):
                row = t * third + r * CHIPS
                ref[pl.ds(r * fresh + t * CHIPS, CHIPS), :] = value[row : row + CHIPS]

    put(q_ref, turn(acc[:, :width]))
    put(k_ref, turn(acc[:, width : 2 * width]))
    put(v_ref, acc[:, 2 * width :])

    for name in started:
        weight_copy(name).wait_send()
    for s in (1, -1):
        for k in (1, 2, 3, 4):
            for t in range(THIRDS):
                if k < 4 or t in dict(last_parts(s)):
                    z_copy(k, s, t).wait_send()
    swap.wait_send()

    @pl.loop(1, CHIPS)
    def _(d):
        first(d).wait_send()
        second(d).wait_send()


def project(lengths, x, w, group_of, gain, bias, col_bias):
    tokens, part = x.shape
    depth, cols = w.shape
    width = cols // 3
    lanes = tokens * part // (CHIPS * 8)
    f32, bf16 = jnp.float32, jnp.bfloat16
    out = jax.ShapeDtypeStruct((tokens, width), bf16)
    vmem = pl.BlockSpec(memory_space=pltpu.VMEM)
    smem = pl.BlockSpec(memory_space=pltpu.SMEM)
    anywhere = pl.BlockSpec(memory_space=pl.ANY)
    message = pltpu.VMEM((CHIPS, 8, lanes), bf16)
    wide = pltpu.VMEM((tokens, 128), f32)
    pairs = pltpu.SemaphoreType.DMA((CHIPS,))
    copies = pltpu.SemaphoreType.DMA((len(NUMBER),))
    return pl.pallas_call(
        project_kernel,
        out_shape=(out, out, out),
        in_specs=[smem, anywhere, anywhere, vmem, vmem, vmem, vmem],
        out_specs=(vmem, vmem, vmem),
        scratch_shapes=[
            pltpu.VMEM((tokens, part), bf16),
            pltpu.VMEM((depth, cols), bf16),
            pltpu.VMEM((CHIPS // 2, 4 * depth, cols), bf16),
            pltpu.VMEM((DEPTH, tokens, part), bf16),
            pltpu.VMEM((DEPTH, tokens, part), bf16),
            pltpu.VMEM((tokens, cols), f32),
            wide,
            wide,
            wide,
            wide,
            wide,
            pltpu.VMEM((8, part * DEPTH), f32),
            pltpu.VMEM((8, part * DEPTH), f32),
            message,
            message,
            message,
            message,
            message,
            pltpu.SemaphoreType.DMA((2,)),
            copies,
            copies,
            pairs,
            pairs,
            pairs,
            pairs,
        ],
        compiler_params=pltpu.CompilerParams(
            collective_id=0, has_side_effects=True, vmem_limit_bytes=VMEM_BYTES
        ),
    )(lengths, x, w, group_of, gain, bias, col_bias)


def per_device(
    arrivals, group_of, lengths, page_table, ln_gain, ln_bias, w_qkv, qkv_bias, key_pool, value_pool
):
    req_count, fresh, part = arrivals.shape
    x = arrivals.reshape(req_count * fresh, part)
    q, k, v = project(lengths, x, w_qkv, group_of, ln_gain, ln_bias, qkv_bias)
    outs = attention(lengths, page_table, q, k, v, key_pool, value_pool)
    return tuple(a.reshape(req_count, fresh, -1) for a in outs)


def solution(mesh):
    in_specs = (
        P("req", None, "wgt"),
        P(),
        P("req"),
        P("req", None),
        P(),
        P(),
        P("req", "wgt"),
        P("wgt"),
        P("req", None, "wgt"),
        P("req", None, "wgt"),
    )
    out_specs = (P("req", None, "wgt"), P("req", None, "wgt"), P("req", None, "wgt"))
    return jax.shard_map(
        per_device, mesh=mesh, in_specs=in_specs, out_specs=out_specs, check_vma=False
    )
```

time: 111 us -> 88.9 us (0.80)
  the two profiles are of different devices: /device:TPU:2 before, /device:TPU:1 now
where the time goes in v3:
time: 88.9 us; the launch traced here: 88.7 us
  Pallas kernels  88.1 us (99%)
    pallas_call x1, Pallas kernels, project(): pl.pallas_call(project_kernel, out_shape=(out, out, out), in_specs=[smem,...  77.1 us
    pallas_call x1, Pallas kernels, attention(): pl.pallas_call(attention_kernel, out_shape=(out, out, out), in_specs=[sme...  10.9 us

profile of v3, /device:TPU:1, one launch (start us, length us, event | category | flops | bytes accessed | tf_op | source)
XLA Modules:
  0.0 88.7 jit_solution(4693331640652961166)
XLA Ops:
  0.6 77.1 %shard_map.121 = (bf16[192,384]{1,0:T(8,128)(2,1)}, bf16[192,384]{1,0:T(8,128)(2,1)}, bf16[192,384]{1,0:T(8,128)(2,1)}) custom-call(s32[4]{0:T(128)} %lengths.3, bf16[192,768]{1,0:T(8,128)(2,1)} %bitcast.4, bf16[192,1152]{1,0:T(8,128)(2,1)} %w_hbm.1, s32[128]{0:T(128)} %group_ref.1, bf16[6144]{0:T(1024)(128)(2,1)} %gain_ref.1, bf16[6144]{0:T(1024)(128)(2,1)} %bias_ref.1, ...), custom_call_target="tpu_custom_call" | custom-call | tf_op jit(solution)/shard_map/pallas_call | solution.py:558
  77.8 10.9 %shard_map.122 = (bf16[192,384]{1,0:T(8,128)(2,1)}, bf16[192,384]{1,0:T(8,128)(2,1)}, bf16[192,384]{1,0:T(8,128)(2,1)}) custom-call(s32[4]{0:T(128)} %lengths.3, s32[4,16]{1,0:T(4,128)} %table.1, bf16[192,384]{1,0:T(8,128)(2,1)} %get-tuple-element.9.q_ref, bf16[192,384]{1,0:T(8,128)(2,1)} %get-tuple-element.10.k_ref, ...), custom_call_target="tpu_custom_call" | custom-call | tf_op jit(solution)/shard_map/pallas_call | solution.py:123

commit v4 on v3

--- a/solution.py
+++ b/solution.py
@@ -166,6 +166,17 @@
 NUMBER = copy_numbers()
 
 
+def arrivals_in_order():
+    rows = lambda du: [("row", h, du, s) for h in (1, 0) for s in (1, -1)]
+    rows_on = lambda du: [("row on", 1, du), ("row on", 0, du)]
+    thirds = lambda k, *ts: [("z", k, s, t) for t in ts for s in (1, -1)]
+    order = rows(0) + thirds(1, 0) + [("own on", 0), ("own on", 1)] + thirds(1, 1, 2)
+    order += rows(-1) + thirds(2, 0, 1, 2) + rows(1) + thirds(3, 0) + rows_on(0) + thirds(3, 1, 2)
+    order += rows(2) + [("z", 4, -1, 1), ("z", 4, 1, 0), ("z", 4, 1, 1), ("z", 4, -1, 2)]
+    order += rows_on(-1) + ["row 0"] + rows_on(1) + ["row -1"] + rows_on(2) + ["row 1", "row 2"]
+    return order
+
+
 def project_kernel(
     lengths, x_hbm, w_hbm, group_ref, gain_ref, bias_ref, col_bias_ref, q_ref, k_ref, v_ref,
     x_ref, w_ref, weights, slabs, normed, acc, cosines, sines, pivot, sums, squares, gains, biases,
@@ -374,10 +385,16 @@
     for h in (0, 1):
         for s in (1, -1):
             arrive("own", h, s)
+    for h in (0, 1):
+        for s in (1, -1):
             start("own on", h, s)
+    for h in (0, 1):
+        for s in (1, -1):
+            start("core", h, -s, 0)
+    for s in (1, -1):
+        for h in (0, 1):
             start("row", h, -s, 1)
             start("row", h, -s, -1)
-            start("core", h, -s, 0)
 
     @pl.loop(1, CHIPS)
     def _(d):
@@ -418,8 +435,8 @@
     sums[...] = jnp.zeros_like(sums)
     squares[...] = jnp.zeros_like(squares)
 
-    def add_sums(number):
-        @pl.loop(0, tokens, step=32)
+    def add_sums(number, t):
+        @pl.loop(t * third, (t + 1) * third, step=32)
         def _(start_row):
             mine = pl.ds(pl.multiple_of(start_row, 32), 32)
             origin, total, square = pivot[mine, :], sums[mine, :], squares[mine, :]
@@ -430,74 +447,26 @@
             sums[mine, :] = total
             squares[mine, :] = square
 
-    def z_step(k):
-        if k < 4:
-            for t in range(THIRDS):
-                for s in (1, -1):
-                    z_copy(k, s, t).wait_recv()
-                    if k < 3 or t in dict(last_parts(s)):
-                        z_copy(k + 1, s, t).start()
-            add_sums((z - k + DEPTH) % DEPTH)
-            add_sums((z + k) % DEPTH)
-        else:
-            for s in (1, -1):
-                for t, _ in last_parts(s):
-                    z_copy(4, s, t).wait_recv()
-            add_sums((z + 4) % DEPTH)
-
-    def rows_step(du):
-        for h in (0, 1):
-            for s in (1, -1):
-                arrive("row", h, du, s)
-                start("row on", h, du, s)
-                start("core", h, du, -s)
-
-    for h in (0, 1):
-        for s in (1, -1):
-            arrive("own on", h, s)
-        start("row", h, 2, 1)
-        start("row", h, 2, -1)
-        start("core", h, 2, 0)
-
-    add_sums(z)
-    z_step(1)
-    rows_step(0)
-    z_step(2)
-    rows_step(-1)
-    z_step(3)
-    rows_step(1)
-    z_step(4)
-
-    def normalise(start_row):
-        mine = pl.ds(pl.multiple_of(start_row, 32), 32)
-        shift = jnp.sum(sums[mine, :], axis=1, keepdims=True) * (1.0 / model_width)
-        square = jnp.sum(squares[mine, :], axis=1, keepdims=True) * (1.0 / model_width)
-        inv = jnp.broadcast_to(lax.rsqrt(jnp.maximum(square - shift * shift, 0.0) + EPS), (32, 128))
-        mean = pivot[mine, :] + shift
-        for j in range(model_width // 128):
-            w, lanes = j * 128 // part, slice(j * 128 % part, j * 128 % part + 128)
-            value = (slabs[w, mine, lanes].astype(f32) - mean) * inv
-            value = value.reshape(4, 8, 128) * gains[:, j * 128 : (j + 1) * 128][None]
-            value = value + biases[:, j * 128 : (j + 1) * 128][None]
-            normed[w, mine, lanes] = value.reshape(32, 128).astype(bf16)
-
-    pl.loop(0, tokens, step=32)(normalise)
-
-    rows_step(2)
-
-    def far(h, du):
-        for s in (1, -1):
-            arrive("row on", h, du, s)
-        start("core", h, du, 2)
+    def normalise(t):
+        @pl.loop(t * third, (t + 1) * third, step=32)
+        def _(start_row):
+            mine = pl.ds(pl.multiple_of(start_row, 32), 32)
+            shift = jnp.sum(sums[mine, :], axis=1, keepdims=True) * (1.0 / model_width)
+            square = jnp.sum(squares[mine, :], axis=1, keepdims=True) * (1.0 / model_width)
+            inv = lax.rsqrt(jnp.maximum(square - shift * shift, 0.0) + EPS)
+            inv = jnp.broadcast_to(inv, (32, 128))
+            mean = pivot[mine, :] + shift
+            for j in range(model_width // 128):
+                w, lanes = j * 128 // part, slice(j * 128 % part, j * 128 % part + 128)
+                value = (slabs[w, mine, lanes].astype(f32) - mean) * inv
+                value = value.reshape(4, 8, 128) * gains[:, j * 128 : (j + 1) * 128][None]
+                value = value + biases[:, j * 128 : (j + 1) * 128][None]
+                normed[w, mine, lanes] = value.reshape(32, 128).astype(bf16)
 
     def from_core(h, du, dv):
         remote(("core", h, du, dv), block(h, du, dv, c=1 - core), partner).wait_recv()
 
-    for dy in OFFSETS:
-        far(1, dy)
-        if dy == 2:
-            for dx in OFFSETS:
-                far(0, dx)
+    def multiply(dy):
         for dx in OFFSETS:
             from_core(0, dx, dy)
             from_core(1, dy, dx)
@@ -506,6 +475,42 @@
         @pl.loop(first_pair, first_pair + 2)
         def _(pair):
             acc[...] += jnp.dot(normed[pair], weights[pair], preferred_element_type=f32)
+
+    for t in range(THIRDS):
+        add_sums(z, t)
+
+    seen = set()
+    for event in arrivals_in_order():
+        seen.add(event)
+        if event[0] == "own on":
+            h = event[1]
+            arrive("own on", h, 1)
+            arrive("own on", h, -1)
+            start("row", h, 2, 1)
+            start("row", h, 2, -1)
+            start("core", h, 2, 0)
+        elif event[0] == "row":
+            arrive(*event)
+            _, h, du, s = event
+            start("row on", h, du, s)
+            start("core", h, du, -s)
+        elif event[0] == "row on":
+            _, h, du = event
+            arrive("row on", h, du, 1)
+            arrive("row on", h, du, -1)
+            start("core", h, du, 2)
+        elif event[0] == "z":
+            _, k, s, t = event
+            z_copy(k, s, t).wait_recv()
+            if k < 3 or (k == 3 and t in dict(last_parts(s))):
+                z_copy(k + 1, s, t).start()
+            if k < 4:
+                add_sums((z - k * s + DEPTH) % DEPTH, t)
+            elif all(("z", 4, d, t) in seen for d in (1, -1) if t in dict(last_parts(d))):
+                add_sums((z + 4) % DEPTH, t)
+                normalise(t)
+        else:
+            multiply(int(event.split()[1]))
 
     def turn(value):
         lanes = iota((1, width), 1) % HEAD

time: 88.9 us -> 71.1 us (0.80)
  Pallas kernels: 88.1 us -> 70.3 us
    pallas_call x1, Pallas kernels: 77.1 us -> 60.6 us  [project(): pl.pallas_call(project_kernel, out_shape=(out, out, out), in_specs=[smem,...]
    pallas_call x1, Pallas kernels: 10.9 us -> 9.73 us  [attention(): pl.pallas_call(attention_kernel, out_shape=(out, out, out), in_specs=[sme...]
where the time goes in v4:
time: 71.1 us; the launch traced here: 70.9 us
  Pallas kernels  70.3 us (99%)
    pallas_call x1, Pallas kernels, project(): pl.pallas_call(project_kernel, out_shape=(out, out, out), in_specs=[smem,...  60.6 us
    pallas_call x1, Pallas kernels, attention(): pl.pallas_call(attention_kernel, out_shape=(out, out, out), in_specs=[sme...  9.73 us

profile of v4, /device:TPU:1, one launch (start us, length us, event | category | flops | bytes accessed | tf_op | source)
XLA Modules:
  0.0 70.9 jit_solution(11599207647952713871)
XLA Ops:
  0.6 60.6 %shard_map.121 = (bf16[192,384]{1,0:T(8,128)(2,1)}, bf16[192,384]{1,0:T(8,128)(2,1)}, bf16[192,384]{1,0:T(8,128)(2,1)}) custom-call(s32[4]{0:T(128)} %lengths.3, bf16[192,768]{1,0:T(8,128)(2,1)} %bitcast.4, bf16[192,1152]{1,0:T(8,128)(2,1)} %w_hbm.1, s32[128]{0:T(128)} %group_ref.1, bf16[6144]{0:T(1024)(128)(2,1)} %gain_ref.1, bf16[6144]{0:T(1024)(128)(2,1)} %bias_ref.1, ...), custom_call_target="tpu_custom_call" | custom-call | tf_op jit(solution)/shard_map/pallas_call | solution.py:563
  61.2 9.7 %shard_map.122 = (bf16[192,384]{1,0:T(8,128)(2,1)}, bf16[192,384]{1,0:T(8,128)(2,1)}, bf16[192,384]{1,0:T(8,128)(2,1)}) custom-call(s32[4]{0:T(128)} %lengths.3, s32[4,16]{1,0:T(4,128)} %table.1, bf16[192,384]{1,0:T(8,128)(2,1)} %get-tuple-element.9.q_ref, bf16[192,384]{1,0:T(8,128)(2,1)} %get-tuple-element.10.k_ref, ...), custom_call_target="tpu_custom_call" | custom-call | tf_op jit(solution)/shard_map/pallas_call | solution.py:123

commit v5 on v4

--- a/solution.py
+++ b/solution.py
@@ -17,7 +17,7 @@
 
 def attention_kernel(
     lengths, table, q_ref, k_ref, v_ref, key_pool, value_pool, out_ref, nk_ref, nv_ref,
-    kbuf, vbuf, scores, mixed, sems,
+    kbuf, vbuf, queries, scores, peaks, offsets, totals, mixed, work, sems,
 ):
     f32, bf16 = jnp.float32, jnp.bfloat16
     req_count, maxp = table.shape
@@ -29,23 +29,27 @@
     factor = math.log2(math.e) / math.sqrt(HEAD)
     low = -1e30
 
-    def chunks_of(r):
-        return (lengths[r] + (span - 1)) // span
-
-    def key_copy(r, p):
-        slot = r * maxp + p
-        return pltpu.make_async_copy(key_pool.at[table[r, p]], kbuf.at[slot], sems.at[0, slot])
-
-    def value_copy(r, p):
-        slot = r * maxp + p
-        return pltpu.make_async_copy(value_pool.at[table[r, p]], vbuf.at[slot], sems.at[1, slot])
-
+    count = 0
     for r in range(req_count):
-
-        @pl.loop(0, chunks_of(r) * CHUNK_PAGES)
-        def _(p):
-            key_copy(r, p).start()
-            value_copy(r, p).start()
+        chunks = (lengths[r] + (span - 1)) // span
+
+        @pl.loop(0, chunks)
+        def _(n):
+            i = count + n
+            work[0, i] = r
+            work[1, i] = n
+            for p in range(CHUNK_PAGES):
+                number, slot = table[r, n * CHUNK_PAGES + p], i * CHUNK_PAGES + p
+                pltpu.make_async_copy(key_pool.at[number], kbuf.at[slot], sems.at[0, i]).start()
+                pltpu.make_async_copy(value_pool.at[number], vbuf.at[slot], sems.at[1, i]).start()
+
+        count = count + chunks
+
+    def pages(i):
+        return pl.ds(i * CHUNK_PAGES, CHUNK_PAGES)
+
+    def wait(pool, buffer, kind, i):
+        pltpu.make_async_copy(pool.at[pl.ds(0, CHUNK_PAGES)], buffer.at[pages(i)], sems.at[kind, i]).wait()
 
     nk_ref[...] = k_ref[...]
     nv_ref[...] = v_ref[...]
@@ -62,52 +66,77 @@
         return folded
 
     across = (((1,), (1,)), ((), ()))
-    queries, fresh_scores, fresh_peaks = [], [], []
+    fresh_scores = []
     for r in range(req_count):
         mine = pl.ds(r * fresh, fresh)
         query = jnp.concatenate([q_ref[mine, :]] * heads, axis=0)
         query = jnp.where(own_head, query, jnp.zeros_like(query))
+        queries[r] = query
         own = lax.dot_general(query, k_ref[mine, :], across, preferred_element_type=f32)
         own = jnp.where(causal, own, low)
-        queries.append(query)
         fresh_scores.append(own)
-        fresh_peaks.append(jnp.max(own, axis=1, keepdims=True))
-
+        peaks[r] = jnp.broadcast_to(jnp.max(own, axis=1, keepdims=True), (rows, 128))
+        totals[r] = jnp.zeros((rows, 128), f32)
+
+    def over_chunks(step):
+        @pl.loop(0, count // 2)
+        def _(j):
+            step((2 * j, 2 * j + 1))
+
+        @pl.when(count % 2 == 1)
+        def _():
+            step((count - 1,))
+
+    def first(chunks):
+        for i in chunks:
+            wait(key_pool, kbuf, 0, i)
+        values = []
+        for i in chunks:
+            r, n = work[0, i], work[1, i]
+            keys = kbuf[pages(i)].reshape(span, width)
+            value = lax.dot_general(queries[r], keys, across, preferred_element_type=f32)
+            values.append(value + jnp.where(column < lengths[r] - n * span, 0.0, low))
+        for i, value in zip(chunks, values):
+            r = work[0, i]
+            scores[i] = value
+            peaks[r] = jnp.maximum(peaks[r], fold(value, jnp.maximum))
+
+    over_chunks(first)
+
+    fresh_totals = []
     for r in range(req_count):
         mine = pl.ds(r * fresh, fresh)
-        query, length = queries[r], lengths[r]
-
-        def first(n, peak):
-            for p in range(CHUNK_PAGES):
-                key_copy(r, n * CHUNK_PAGES + p).wait()
-            keys = kbuf[pl.ds(r * maxp + n * CHUNK_PAGES, CHUNK_PAGES)].reshape(span, width)
-            value = lax.dot_general(query, keys, across, preferred_element_type=f32)
-            value = value + jnp.where(column < length - n * span, 0.0, low)
-            scores[n] = value
-            return jnp.maximum(peak, fold(value, jnp.maximum))
-
-        peak = lax.fori_loop(0, chunks_of(r), first, jnp.full((rows, 128), low, f32))
-        peak = jnp.maximum(jnp.max(peak, axis=1, keepdims=True), fresh_peaks[r])
-        offset = peak * factor
+        offset = jnp.max(peaks[r], axis=1, keepdims=True) * factor
+        offsets[r] = jnp.broadcast_to(offset, (rows, 128))
         weights = jnp.exp2(fresh_scores[r] * factor - offset)
-        mixed[...] = jnp.dot(weights.astype(bf16), v_ref[mine, :], preferred_element_type=f32)
-        fresh_total = jnp.sum(weights, axis=1, keepdims=True)
-
-        def second(n, total):
-            for p in range(CHUNK_PAGES):
-                value_copy(r, n * CHUNK_PAGES + p).wait()
-            values = vbuf[pl.ds(r * maxp + n * CHUNK_PAGES, CHUNK_PAGES)].reshape(span, width)
-            weights = jnp.exp2(scores[n] * factor - offset)
-            mixed[...] += jnp.dot(weights.astype(bf16), values, preferred_element_type=f32)
-            return total + fold(weights, jnp.add)
-
-        total = lax.fori_loop(0, chunks_of(r), second, jnp.zeros((rows, 128), f32))
-        total = jnp.sum(total, axis=1, keepdims=True) + fresh_total
-        part = jnp.where(own_head, mixed[...] * (1.0 / total), 0.0)
+        mixed[r] = jnp.dot(weights.astype(bf16), v_ref[mine, :], preferred_element_type=f32)
+        fresh_totals.append(jnp.sum(weights, axis=1, keepdims=True))
+
+    def second(chunks):
+        for i in chunks:
+            wait(value_pool, vbuf, 1, i)
+        parts = []
+        for i in chunks:
+            r = work[0, i]
+            values = vbuf[pages(i)].reshape(span, width)
+            offset = jnp.concatenate([offsets[r]] * (span // 128), axis=1)
+            weights = jnp.exp2(scores[i] * factor - offset)
+            part = jnp.dot(weights.astype(bf16), values, preferred_element_type=f32)
+            parts.append((part, fold(weights, jnp.add)))
+        for i, (part, total) in zip(chunks, parts):
+            r = work[0, i]
+            mixed[r] += part
+            totals[r] += total
+
+    over_chunks(second)
+
+    for r in range(req_count):
+        total = jnp.sum(totals[r], axis=1, keepdims=True) + fresh_totals[r]
+        part = jnp.where(own_head, mixed[r] * (1.0 / total), 0.0)
         summed = part[:fresh]
         for h in range(1, heads):
             summed = summed + part[h * fresh : (h + 1) * fresh]
-        out_ref[mine, :] = summed.astype(out_ref.dtype)
+        out_ref[pl.ds(r * fresh, fresh), :] = summed.astype(out_ref.dtype)
 
 
 def attention(lengths, table, q, k, v, key_pool, value_pool):
@@ -115,8 +144,10 @@
     page = key_pool.shape[1]
     req_count, maxp = table.shape
     slots = req_count * maxp
+    chunks = slots // CHUNK_PAGES
     wide = width // HEAD * (rows // req_count)
-    out = jax.ShapeDtypeStruct((rows, width), jnp.bfloat16)
+    f32, bf16 = jnp.float32, jnp.bfloat16
+    out = jax.ShapeDtypeStruct((rows, width), bf16)
     vmem = pl.BlockSpec(memory_space=pltpu.VMEM)
     smem = pl.BlockSpec(memory_space=pltpu.SMEM)
     anywhere = pl.BlockSpec(memory_space=pl.ANY)
@@ -126,11 +157,16 @@
         in_specs=[smem, smem, vmem, vmem, vmem, anywhere, anywhere],
         out_specs=(vmem, vmem, vmem),
         scratch_shapes=[
-            pltpu.VMEM((slots, page, width), jnp.bfloat16),
-            pltpu.VMEM((slots, page, width), jnp.bfloat16),
-            pltpu.VMEM((maxp // CHUNK_PAGES, wide, CHUNK_PAGES * page), jnp.float32),
-            pltpu.VMEM((wide, width), jnp.float32),
-            pltpu.SemaphoreType.DMA((2, slots)),
+            pltpu.VMEM((slots, page, width), bf16),
+            pltpu.VMEM((slots, page, width), bf16),
+            pltpu.VMEM((req_count, wide, width), bf16),
+            pltpu.VMEM((chunks, wide, CHUNK_PAGES * page), f32),
+            pltpu.VMEM((req_count, wide, 128), f32),
+            pltpu.VMEM((req_count, wide, 128), f32),
+            pltpu.VMEM((req_count, wide, 128), f32),
+            pltpu.VMEM((req_count, wide, width), f32),
+            pltpu.SMEM((2, chunks), jnp.int32),
+            pltpu.SemaphoreType.DMA((2, chunks)),
         ],
         compiler_params=pltpu.CompilerParams(vmem_limit_bytes=VMEM_BYTES),
     )(lengths, table, q, k, v, key_pool, value_pool)
@@ -159,11 +195,16 @@
     for s in (1, -1):
         names += [("z", k, s, t) for k in (1, 2, 3) for t in range(THIRDS)]
         names += [("z", 4, s, t) for t, _ in last_parts(s)]
-    names.append(("swap",))
+    names += [("swap",), ("first",), ("second",)]
     return {name: number for number, name in enumerate(names)}
 
 
 NUMBER = copy_numbers()
+SENDS = ("own", "own on", "row", "row on", "core", "z", "z last", "swap", "first", "second")
+
+
+def send_number(name):
+    return SENDS.index("z last" if name[:2] == ("z", 4) else name[0])
 
 
 def arrivals_in_order():
@@ -173,14 +214,14 @@
     order = rows(0) + thirds(1, 0) + [("own on", 0), ("own on", 1)] + thirds(1, 1, 2)
     order += rows(-1) + thirds(2, 0, 1, 2) + rows(1) + thirds(3, 0) + rows_on(0) + thirds(3, 1, 2)
     order += rows(2) + [("z", 4, -1, 1), ("z", 4, 1, 0), ("z", 4, 1, 1), ("z", 4, -1, 2)]
-    order += rows_on(-1) + ["row 0"] + rows_on(1) + ["row -1"] + rows_on(2) + ["row 1", "row 2"]
+    order += rows_on(-1) + ["row 0"] + rows_on(1) + ["row -1"] + rows_on(2) + ["row 1", "near 2", "far 2"]
     return order
 
 
 def project_kernel(
     lengths, x_hbm, w_hbm, group_ref, gain_ref, bias_ref, col_bias_ref, q_ref, k_ref, v_ref,
     x_ref, w_ref, weights, slabs, normed, acc, cosines, sines, pivot, sums, squares, gains, biases,
-    out1, in1, swapped, out2, in2, load, send, recv, send1, recv1, send2, recv2,
+    out1, in1, swapped, out2, in2, load, send, recv,
 ):
     f32, bf16, i32 = jnp.float32, jnp.bfloat16, jnp.int32
     tokens, part = x_ref.shape
@@ -210,8 +251,7 @@
 
     barrier = pltpu.get_barrier_semaphore()
 
-    @pl.loop(1, CHIPS)
-    def _(d):
+    for d in range(1, CHIPS):
         pl.semaphore_signal(barrier, 1, device_id=device((chip + d) % CHIPS), device_id_type=MESH)
 
     pl.semaphore_signal(barrier, 1, device_id=partner, device_id_type=MESH)
@@ -231,25 +271,26 @@
 
     pl.semaphore_wait(barrier, CHIPS - 1 + 3)
 
-    def spread(source, target, send_sems, recv_sems):
-        def copy(d):
+    def spread(name, source, target):
+        for d in range(1, CHIPS):
             other = (chip + d) % CHIPS
-            return pltpu.make_async_remote_copy(
-                src_ref=source.at[other],
-                dst_ref=target.at[chip],
-                send_sem=send_sems.at[d],
-                recv_sem=recv_sems.at[d],
-                device_id=device(other),
-                device_id_type=MESH,
-            )
-
-        return copy
-
-    first, second = spread(out1, in1, send1, recv1), spread(out2, in2, send2, recv2)
-
-    @pl.loop(1, CHIPS)
-    def _(d):
-        first(d).start()
+            remote((name,), source.at[other], device(other), target.at[chip]).start()
+
+    def gathered(name, target):
+        ref = target.at[pl.ds(0, CHIPS - 1)]
+        remote((name,), ref, partner).wait_recv()
+
+    def remote(name, ref, target, dst=None):
+        return pltpu.make_async_remote_copy(
+            src_ref=ref,
+            dst_ref=ref if dst is None else dst,
+            send_sem=send.at[send_number(name)],
+            recv_sem=recv.at[NUMBER[name]],
+            device_id=target,
+            device_id_type=MESH,
+        )
+
+    spread("first", out1, in1)
 
     def by_kind(value):
         heads = range(width // HEAD)
@@ -268,16 +309,6 @@
     load_w.wait()
     own_pair, own_row = place(chip, core)
     weights[own_pair, pl.ds(pl.multiple_of(own_row, 64), depth), :] = by_kind(w_ref[...])
-
-    def remote(name, ref, target, dst=None):
-        return pltpu.make_async_remote_copy(
-            src_ref=ref,
-            dst_ref=ref if dst is None else dst,
-            send_sem=send.at[NUMBER[name]],
-            recv_sem=recv.at[NUMBER[name]],
-            device_id=target,
-            device_id_type=MESH,
-        )
 
     where = {0: (x, y), 1: (y, x)}
 
@@ -307,11 +338,8 @@
         du, dv = name[2], name[3]
         return remote(name, block(h, du, dv), partner)
 
-    started = []
-
     def start(*name):
         weight_copy(name).start()
-        started.append(name)
 
     def arrive(*name):
         weight_copy(name).wait_recv()
@@ -338,9 +366,7 @@
 
     pick_own, pick_other = selector(core), selector(1 - core)
 
-    @pl.loop(1, CHIPS)
-    def _(d):
-        first(d).wait_recv()
+    gathered("first", in1)
 
     swap = remote(("swap",), in1, partner, swapped)
     swap.start()
@@ -354,9 +380,7 @@
     out2[...] = mixed.reshape(CHIPS, 8, THIRDS * half).astype(bf16)
     in2[chip] = out2[chip]
 
-    @pl.loop(1, CHIPS)
-    def _(d):
-        second(d).start()
+    spread("second", out2, in2)
 
     for h in (0, 1):
         for s in (1, -1):
@@ -396,9 +420,7 @@
             start("row", h, -s, 1)
             start("row", h, -s, -1)
 
-    @pl.loop(1, CHIPS)
-    def _(d):
-        second(d).wait_recv()
+    gathered("second", in2)
 
     m, n = iota((third, CHIPS * 8), 0), iota((third, CHIPS * 8), 1)
     pieces = flat(in2)
@@ -466,15 +488,21 @@
     def from_core(h, du, dv):
         remote(("core", h, du, dv), block(h, du, dv, c=1 - core), partner).wait_recv()
 
-    def multiply(dy):
+    def multiply_pair(pair):
+        acc[...] += jnp.dot(normed[pair], weights[pair], preferred_element_type=f32)
+
+    def multiply(dy, what):
         for dx in OFFSETS:
-            from_core(0, dx, dy)
-            from_core(1, dy, dx)
+            if (dx == 2 and what != "near") or (dx != 2 and what != "far"):
+                from_core(0, dx, dy)
+                from_core(1, dy, dx)
         first_pair = (y + dy + SIDE) % SIDE * 2
-
-        @pl.loop(first_pair, first_pair + 2)
-        def _(pair):
-            acc[...] += jnp.dot(normed[pair], weights[pair], preferred_element_type=f32)
+        if what == "row":
+            pl.loop(first_pair, first_pair + 2)(multiply_pair)
+        elif what == "near":
+            multiply_pair(first_pair + x // 2)
+        else:
+            multiply_pair(first_pair + 1 - x // 2)
 
     for t in range(THIRDS):
         add_sums(z, t)
@@ -510,40 +538,43 @@
                 add_sums((z + 4) % DEPTH, t)
                 normalise(t)
         else:
-            multiply(int(event.split()[1]))
-
-    def turn(value):
-        lanes = iota((1, width), 1) % HEAD
-        forward, backward = pltpu.roll(value, width - turning, 1), pltpu.roll(value, turning, 1)
-        near = jnp.where(lanes < turning, forward, backward)
-        cosine = jnp.concatenate([cosines[...]] * (width // 128), axis=1)
-        sine = jnp.concatenate([sines[...]] * (width // 128), axis=1)
-        return jnp.where(lanes < ROT, value * cosine + near * sine, value)
-
-    def put(ref, value):
-        value = value.astype(bf16)
-        for t in range(THIRDS):
-            for r in range(req_count):
-                row = t * third + r * CHIPS
-                ref[pl.ds(r * fresh + t * CHIPS, CHIPS), :] = value[row : row + CHIPS]
-
-    put(q_ref, turn(acc[:, :width]))
-    put(k_ref, turn(acc[:, width : 2 * width]))
-    put(v_ref, acc[:, 2 * width :])
-
-    for name in started:
-        weight_copy(name).wait_send()
-    for s in (1, -1):
-        for k in (1, 2, 3, 4):
-            for t in range(THIRDS):
-                if k < 4 or t in dict(last_parts(s)):
-                    z_copy(k, s, t).wait_send()
-    swap.wait_send()
-
-    @pl.loop(1, CHIPS)
-    def _(d):
-        first(d).wait_send()
-        second(d).wait_send()
+            what, dy = event.split()
+            multiply(int(dy), what)
+
+    lanes = iota((1, width), 1) % HEAD
+    rotated = [lanes[:, j * 128 : (j + 1) * 128] for j in range(width // 128)]
+    for t in range(THIRDS):
+        for r in range(req_count):
+            here = pl.ds(t * third + r * CHIPS, CHIPS)
+            there = pl.ds(r * fresh + t * CHIPS, CHIPS)
+            cosine, sine = cosines[here, :], sines[here, :]
+            for kind, ref in enumerate((q_ref, k_ref, v_ref)):
+                for j in range(width // 128):
+                    column = kind * width + j * 128
+                    value = acc[here, column : column + 128]
+                    if kind < 2:
+                        near = jnp.where(
+                            rotated[j] < turning,
+                            pltpu.roll(value, 128 - turning, 1),
+                            pltpu.roll(value, turning, 1),
+                        )
+                        value = jnp.where(rotated[j] < ROT, value * cosine + near * sine, value)
+                    ref[there, j * 128 : (j + 1) * 128] = value.astype(bf16)
+
+    def sent(kind, ref):
+        name = ("z", 4, 1, 0) if kind == "z last" else next(n for n in NUMBER if n[0] == kind)
+        remote(name, ref, partner).wait_send()
+
+    sent("own", weights.at[0, pl.ds(0, 2 * depth), :])
+    sent("own on", weights.at[0, pl.ds(0, depth), :])
+    sent("row", weights.at[pl.ds(0, 2)])
+    sent("row on", weights.at[0])
+    sent("core", weights.at[pl.ds(0, 4)])
+    sent("z", slabs.at[pl.ds(0, 6)])
+    sent("z last", slabs.at[0])
+    sent("swap", in1)
+    sent("first", in1.at[pl.ds(0, CHIPS - 1)])
+    sent("second", in1.at[pl.ds(0, CHIPS - 1)])
 
 
 def project(lengths, x, w, group_of, gain, bias, col_bias):
@@ -558,7 +589,6 @@
     anywhere = pl.BlockSpec(memory_space=pl.ANY)
     message = pltpu.VMEM((CHIPS, 8, lanes), bf16)
     wide = pltpu.VMEM((tokens, 128), f32)
-    pairs = pltpu.SemaphoreType.DMA((CHIPS,))
     copies = pltpu.SemaphoreType.DMA((len(NUMBER),))
     return pl.pallas_call(
         project_kernel,
@@ -585,12 +615,8 @@
             message,
             message,
             pltpu.SemaphoreType.DMA((2,)),
+            pltpu.SemaphoreType.DMA((len(SENDS),)),
             copies,
-            copies,
-            pairs,
-            pairs,
-            pairs,
-            pairs,
         ],
         compiler_params=pltpu.CompilerParams(
             collective_id=0, has_side_effects=True, vmem_limit_bytes=VMEM_BYTES

time: 71.1 us -> 67.3 us (0.947)
  Pallas kernels: 70.3 us -> 66.5 us
    pallas_call x1, Pallas kernels: 60.6 us -> 58.4 us  [project(): pl.pallas_call(project_kernel, out_shape=(out, out, out), in_specs=[smem,...]
    pallas_call x1, Pallas kernels: 9.73 us -> 8.06 us  [attention(): pl.pallas_call(attention_kernel, out_shape=(out, out, out), in_specs=[sme...]
where the time goes in v5:
time: 67.3 us; the launch traced here: 67.1 us
  Pallas kernels  66.5 us (99%)
    pallas_call x1, Pallas kernels, project(): pl.pallas_call(project_kernel, out_shape=(out, out, out), in_specs=[smem,...  58.4 us
    pallas_call x1, Pallas kernels, attention(): pl.pallas_call(attention_kernel, out_shape=(out, out, out), in_specs=[sme...  8.06 us

profile of v5, /device:TPU:1, one launch (start us, length us, event | category | flops | bytes accessed | tf_op | source)
XLA Modules:
  0.0 67.1 jit_solution(18336118916299676432)
XLA Ops:
  0.6 58.4 %shard_map.121 = (bf16[192,384]{1,0:T(8,128)(2,1)}, bf16[192,384]{1,0:T(8,128)(2,1)}, bf16[192,384]{1,0:T(8,128)(2,1)}) custom-call(s32[4]{0:T(128)} %lengths.3, bf16[192,768]{1,0:T(8,128)(2,1)} %bitcast.4, bf16[192,1152]{1,0:T(8,128)(2,1)} %w_hbm.1, s32[128]{0:T(128)} %group_ref.1, bf16[6144]{0:T(1024)(128)(2,1)} %gain_ref.1, bf16[6144]{0:T(1024)(128)(2,1)} %bias_ref.1, ...), custom_call_target="tpu_custom_call" | custom-call | tf_op jit(solution)/shard_map/pallas_call | solution.py:593
  59.1 8.1 %shard_map.122 = (bf16[192,384]{1,0:T(8,128)(2,1)}, bf16[192,384]{1,0:T(8,128)(2,1)}, bf16[192,384]{1,0:T(8,128)(2,1)}) custom-call(s32[4]{0:T(128)} %lengths.3, s32[4,16]{1,0:T(4,128)} %table.1, bf16[192,384]{1,0:T(8,128)(2,1)} %get-tuple-element.9.q_ref, bf16[192,384]{1,0:T(8,128)(2,1)} %get-tuple-element.10.k_ref, ...), custom_call_target="tpu_custom_call" | custom-call | tf_op jit(solution)/shard_map/pallas_call | solution.py:154

commit v6 on v5

--- a/solution.py
+++ b/solution.py
@@ -16,8 +16,8 @@
 
 
 def attention_kernel(
-    lengths, table, q_ref, k_ref, v_ref, key_pool, value_pool, out_ref, nk_ref, nv_ref,
-    kbuf, vbuf, queries, scores, peaks, offsets, totals, mixed, work, sems,
+    lengths, table, q_hbm, k_hbm, v_hbm, key_pool, value_pool, out_hbm, nk_hbm, nv_hbm,
+    q_ref, k_ref, v_ref, out_ref, kbuf, vbuf, queries, scores, peaks, offsets, totals, mixed, work, sems, io,
 ):
     f32, bf16 = jnp.float32, jnp.bfloat16
     req_count, maxp = table.shape
@@ -29,6 +29,13 @@
     factor = math.log2(math.e) / math.sqrt(HEAD)
     low = -1e30
 
+    loads = [
+        pltpu.make_async_copy(source, target, io.at[n])
+        for n, (source, target) in enumerate(((q_hbm, q_ref), (k_hbm, k_ref), (v_hbm, v_ref)))
+    ]
+    for copy in loads:
+        copy.start()
+
     count = 0
     for r in range(req_count):
         chunks = (lengths[r] + (span - 1)) // span
@@ -51,11 +58,21 @@
     def wait(pool, buffer, kind, i):
         pltpu.make_async_copy(pool.at[pl.ds(0, CHUNK_PAGES)], buffer.at[pages(i)], sems.at[kind, i]).wait()
 
-    nk_ref[...] = k_ref[...]
-    nv_ref[...] = v_ref[...]
+    for copy in loads:
+        copy.wait()
+    stores = [
+        pltpu.make_async_copy(k_ref, nk_hbm, io.at[3]),
+        pltpu.make_async_copy(v_ref, nv_hbm, io.at[4]),
+        pltpu.make_async_copy(out_ref, out_hbm, io.at[5]),
+    ]
+    stores[0].start()
+    stores[1].start()
 
     iota = lambda shape, axis: lax.broadcasted_iota(jnp.int32, shape, axis)
-    own_head = iota((rows, width), 1) // HEAD == iota((rows, width), 0) // fresh
+    row_head = iota((rows, 256), 0) // fresh
+    own_head = (iota((rows, 256), 1) + row_head // 2 * 128) // HEAD == row_head
+    half_rows = rows // 2
+    halves = ((slice(0, half_rows), slice(0, 256)), (slice(half_rows, rows), slice(128, 384)))
     causal = iota((rows, fresh), 0) % fresh >= iota((rows, fresh), 1)
     column = iota((1, span), 1)
 
@@ -66,13 +83,29 @@
         return folded
 
     across = (((1,), (1,)), ((), ()))
+
+    def times_keys(query, keys):
+        products = [
+            lax.dot_general(query[group], keys[:, lanes], across, preferred_element_type=f32)
+            for group, lanes in halves
+        ]
+        return jnp.concatenate(products, axis=0)
+
+    def times_values(weights, values):
+        weights = weights.astype(bf16)
+        products = [
+            jnp.dot(weights[group], values[:, lanes], preferred_element_type=f32)
+            for group, lanes in halves
+        ]
+        return jnp.concatenate(products, axis=0)
+
     fresh_scores = []
     for r in range(req_count):
         mine = pl.ds(r * fresh, fresh)
-        query = jnp.concatenate([q_ref[mine, :]] * heads, axis=0)
+        query = jnp.concatenate([q_ref[mine, lanes] for _, lanes in halves for _ in (0, 1)], axis=0)
         query = jnp.where(own_head, query, jnp.zeros_like(query))
         queries[r] = query
-        own = lax.dot_general(query, k_ref[mine, :], across, preferred_element_type=f32)
+        own = times_keys(query, k_ref[mine, :])
         own = jnp.where(causal, own, low)
         fresh_scores.append(own)
         peaks[r] = jnp.broadcast_to(jnp.max(own, axis=1, keepdims=True), (rows, 128))
@@ -94,7 +127,7 @@
         for i in chunks:
             r, n = work[0, i], work[1, i]
             keys = kbuf[pages(i)].reshape(span, width)
-            value = lax.dot_general(queries[r], keys, across, preferred_element_type=f32)
+            value = times_keys(queries[r], keys)
             values.append(value + jnp.where(column < lengths[r] - n * span, 0.0, low))
         for i, value in zip(chunks, values):
             r = work[0, i]
@@ -109,7 +142,7 @@
         offset = jnp.max(peaks[r], axis=1, keepdims=True) * factor
         offsets[r] = jnp.broadcast_to(offset, (rows, 128))
         weights = jnp.exp2(fresh_scores[r] * factor - offset)
-        mixed[r] = jnp.dot(weights.astype(bf16), v_ref[mine, :], preferred_element_type=f32)
+        mixed[r] = times_values(weights, v_ref[mine, :])
         fresh_totals.append(jnp.sum(weights, axis=1, keepdims=True))
 
     def second(chunks):
@@ -121,7 +154,7 @@
             values = vbuf[pages(i)].reshape(span, width)
             offset = jnp.concatenate([offsets[r]] * (span // 128), axis=1)
             weights = jnp.exp2(scores[i] * factor - offset)
-            part = jnp.dot(weights.astype(bf16), values, preferred_element_type=f32)
+            part = times_values(weights, values)
             parts.append((part, fold(weights, jnp.add)))
         for i, (part, total) in zip(chunks, parts):
             r = work[0, i]
@@ -133,10 +166,15 @@
     for r in range(req_count):
         total = jnp.sum(totals[r], axis=1, keepdims=True) + fresh_totals[r]
         part = jnp.where(own_head, mixed[r] * (1.0 / total), 0.0)
-        summed = part[:fresh]
-        for h in range(1, heads):
-            summed = summed + part[h * fresh : (h + 1) * fresh]
-        out_ref[pl.ds(r * fresh, fresh), :] = summed.astype(out_ref.dtype)
+        low_pair = part[:fresh] + part[fresh : 2 * fresh]
+        high_pair = part[2 * fresh : 3 * fresh] + part[3 * fresh :]
+        middle = low_pair[:, 128:] + high_pair[:, :128]
+        value = jnp.concatenate([low_pair[:, :128], middle, high_pair[:, 128:]], axis=1)
+        out_ref[pl.ds(r * fresh, fresh), :] = value.astype(out_ref.dtype)
+
+    stores[2].start()
+    for copy in stores:
+        copy.wait()
 
 
 def attention(lengths, table, q, k, v, key_pool, value_pool):
@@ -148,25 +186,29 @@
     wide = width // HEAD * (rows // req_count)
     f32, bf16 = jnp.float32, jnp.bfloat16
     out = jax.ShapeDtypeStruct((rows, width), bf16)
-    vmem = pl.BlockSpec(memory_space=pltpu.VMEM)
     smem = pl.BlockSpec(memory_space=pltpu.SMEM)
     anywhere = pl.BlockSpec(memory_space=pl.ANY)
     return pl.pallas_call(
         attention_kernel,
         out_shape=(out, out, out),
-        in_specs=[smem, smem, vmem, vmem, vmem, anywhere, anywhere],
-        out_specs=(vmem, vmem, vmem),
+        in_specs=[smem, smem] + [anywhere] * 5,
+        out_specs=(anywhere, anywhere, anywhere),
         scratch_shapes=[
+            pltpu.VMEM((rows, width), bf16),
+            pltpu.VMEM((rows, width), bf16),
+            pltpu.VMEM((rows, width), bf16),
+            pltpu.VMEM((rows, width), bf16),
             pltpu.VMEM((slots, page, width), bf16),
             pltpu.VMEM((slots, page, width), bf16),
-            pltpu.VMEM((req_count, wide, width), bf16),
+            pltpu.VMEM((req_count, wide, 256), bf16),
             pltpu.VMEM((chunks, wide, CHUNK_PAGES * page), f32),
             pltpu.VMEM((req_count, wide, 128), f32),
             pltpu.VMEM((req_count, wide, 128), f32),
             pltpu.VMEM((req_count, wide, 128), f32),
-            pltpu.VMEM((req_count, wide, width), f32),
+            pltpu.VMEM((req_count, wide, 256), f32),
             pltpu.SMEM((2, chunks), jnp.int32),
             pltpu.SemaphoreType.DMA((2, chunks)),
+            pltpu.SemaphoreType.DMA((6,)),
         ],
         compiler_params=pltpu.CompilerParams(vmem_limit_bytes=VMEM_BYTES),
     )(lengths, table, q, k, v, key_pool, value_pool)
@@ -219,8 +261,8 @@
 
 
 def project_kernel(
-    lengths, x_hbm, w_hbm, group_ref, gain_ref, bias_ref, col_bias_ref, q_ref, k_ref, v_ref,
-    x_ref, w_ref, weights, slabs, normed, acc, cosines, sines, pivot, sums, squares, gains, biases,
+    lengths_hbm, x_hbm, w_hbm, group_hbm, gain_hbm, bias_hbm, col_bias_hbm, q_hbm, k_hbm, v_hbm,
+    lengths, x_ref, w_ref, group_ref, gain_ref, bias_ref, col_bias_ref, q_ref, k_ref, v_ref, weights, slabs, normed, acc, cosines, sines, pivot, sums, squares, gains, biases,
     out1, in1, swapped, out2, in2, load, send, recv,
 ):
     f32, bf16, i32 = jnp.float32, jnp.bfloat16, jnp.int32
@@ -244,10 +286,12 @@
 
     partner = device(chip, 1 - core)
 
-    load_x = pltpu.make_async_copy(x_hbm, x_ref, load.at[0])
-    load_w = pltpu.make_async_copy(w_hbm, w_ref, load.at[1])
-    load_x.start()
-    load_w.start()
+    pairs = (
+        (x_hbm, x_ref), (w_hbm, w_ref), (group_hbm, group_ref), (lengths_hbm, lengths),
+        (gain_hbm, gain_ref), (bias_hbm, bias_ref), (col_bias_hbm, col_bias_ref),
+    )
+    loads = [pltpu.make_async_copy(a, b, load.at[n]) for n, (a, b) in enumerate(pairs)]
+    loads[0].start()
 
     barrier = pltpu.get_barrier_semaphore()
 
@@ -258,7 +302,10 @@
     for s in (1, DEPTH - 1):
         pl.semaphore_signal(barrier, 1, device_id=(me, (z + s) % DEPTH), device_id_type=MESH)
 
-    load_x.wait()
+    for copy in loads[1:]:
+        copy.start()
+
+    loads[0].wait()
     m, n = iota((CHIPS * 8, tokens), 0), iota((CHIPS * 8, tokens), 1)
     for t in range(THIRDS):
         take = (m % 8) // 2 * fresh + t * CHIPS + m // 8 == n
@@ -306,7 +353,7 @@
     def place(number, c):
         return number // 2, (number % 2) * (2 * depth) + c * depth
 
-    load_w.wait()
+    loads[1].wait()
     own_pair, own_row = place(chip, core)
     weights[own_pair, pl.ds(pl.multiple_of(own_row, 64), depth), :] = by_kind(w_ref[...])
 
@@ -351,6 +398,7 @@
         start("core", h, 0, 0)
 
     a, b = iota((CHIPS * 8, CHIPS * 8), 0), iota((CHIPS * 8, CHIPS * 8), 1)
+    loads[2].wait()
     groups = group_ref[...].reshape(1, -1)
     group_row = jnp.broadcast_to(groups, a.shape)
     group_col = jnp.sum(jnp.where(a == b, group_row, 0), axis=1, keepdims=True)
@@ -386,6 +434,8 @@
         for s in (1, -1):
             start("row", h, 0, s)
 
+    for copy in loads[3:]:
+        copy.wait()
     gains[...] = jnp.broadcast_to(gain_ref[...].astype(f32).reshape(1, -1), gains.shape)
     biases[...] = jnp.broadcast_to(bias_ref[...].astype(f32).reshape(1, -1), biases.shape)
     acc[...] = jnp.broadcast_to(by_kind(col_bias_ref[...].astype(f32).reshape(1, -1)), acc.shape)
@@ -561,6 +611,13 @@
                         value = jnp.where(rotated[j] < ROT, value * cosine + near * sine, value)
                     ref[there, j * 128 : (j + 1) * 128] = value.astype(bf16)
 
+    results = [
+        pltpu.make_async_copy(a, b, load.at[n])
+        for n, (a, b) in enumerate(((q_ref, q_hbm), (k_ref, k_hbm), (v_ref, v_hbm)))
+    ]
+    for copy in results:
+        copy.start()
+
     def sent(kind, ref):
         name = ("z", 4, 1, 0) if kind == "z last" else next(n for n in NUMBER if n[0] == kind)
         remote(name, ref, partner).wait_send()
@@ -575,6 +632,8 @@
     sent("swap", in1)
     sent("first", in1.at[pl.ds(0, CHIPS - 1)])
     sent("second", in1.at[pl.ds(0, CHIPS - 1)])
+    for copy in results:
+        copy.wait()
 
 
 def project(lengths, x, w, group_of, gain, bias, col_bias):
@@ -584,8 +643,6 @@
     lanes = tokens * part // (CHIPS * 8)
     f32, bf16 = jnp.float32, jnp.bfloat16
     out = jax.ShapeDtypeStruct((tokens, width), bf16)
-    vmem = pl.BlockSpec(memory_space=pltpu.VMEM)
-    smem = pl.BlockSpec(memory_space=pltpu.SMEM)
     anywhere = pl.BlockSpec(memory_space=pl.ANY)
     message = pltpu.VMEM((CHIPS, 8, lanes), bf16)
     wide = pltpu.VMEM((tokens, 128), f32)
@@ -593,11 +650,19 @@
     return pl.pallas_call(
         project_kernel,
         out_shape=(out, out, out),
-        in_specs=[smem, anywhere, anywhere, vmem, vmem, vmem, vmem],
-        out_specs=(vmem, vmem, vmem),
+        in_specs=[anywhere] * 7,
+        out_specs=(anywhere, anywhere, anywhere),
         scratch_shapes=[
+            pltpu.SMEM(lengths.shape, jnp.int32),
             pltpu.VMEM((tokens, part), bf16),
             pltpu.VMEM((depth, cols), bf16),
+            pltpu.VMEM(group_of.shape, jnp.int32),
+            pltpu.VMEM(gain.shape, bf16),
+            pltpu.VMEM(bias.shape, bf16),
+            pltpu.VMEM(col_bias.shape, bf16),
+            pltpu.VMEM((tokens, width), bf16),
+            pltpu.VMEM((tokens, width), bf16),
+            pltpu.VMEM((tokens, width), bf16),
             pltpu.VMEM((CHIPS // 2, 4 * depth, cols), bf16),
             pltpu.VMEM((DEPTH, tokens, part), bf16),
             pltpu.VMEM((DEPTH, tokens, part), bf16),
@@ -614,7 +679,7 @@
             message,
             message,
             message,
-            pltpu.SemaphoreType.DMA((2,)),
+            pltpu.SemaphoreType.DMA((7,)),
             pltpu.SemaphoreType.DMA((len(SENDS),)),
             copies,
         ],

time: 67.3 us -> 65.2 us (0.969)
  Pallas kernels: 66.5 us -> 64.4 us
    pallas_call x1, Pallas kernels: 8.06 us -> 6.79 us  [attention(): pl.pallas_call(attention_kernel, out_shape=(out, out, out), in_specs=[sme...]
    pallas_call x1, Pallas kernels: 58.4 us -> 57.7 us  [project(): pl.pallas_call(project_kernel, out_shape=(out, out, out), in_specs=[anywh...]
where the time goes in v6:
time: 65.2 us; the launch traced here: 65.1 us
  Pallas kernels  64.4 us (99%)
    pallas_call x1, Pallas kernels, project(): pl.pallas_call(project_kernel, out_shape=(out, out, out), in_specs=[anywh...  57.7 us
    pallas_call x1, Pallas kernels, attention(): pl.pallas_call(attention_kernel, out_shape=(out, out, out), in_specs=[sme...  6.79 us

profile of v6, /device:TPU:1, one launch (start us, length us, event | category | flops | bytes accessed | tf_op | source)
XLA Modules:
  0.0 65.1 jit_solution(6243790753185960309)
XLA Ops:
  0.6 57.7 %shard_map.121 = (bf16[192,384]{1,0:T(8,128)(2,1)}, bf16[192,384]{1,0:T(8,128)(2,1)}, bf16[192,384]{1,0:T(8,128)(2,1)}) custom-call(s32[4]{0:T(128)} %lengths.1, bf16[192,768]{1,0:T(8,128)(2,1)} %bitcast.4, bf16[192,1152]{1,0:T(8,128)(2,1)} %w_hbm.1, s32[128]{0:T(128)} %group_hbm.1, bf16[6144]{0:T(1024)(128)(2,1)} %gain_hbm.1, bf16[6144]{0:T(1024)(128)(2,1)} %bias_hbm.1, ...), custom_call_target="tpu_custom_call" | custom-call | tf_op jit(solution)/shard_map/pallas_call | solution.py:650
  58.3 6.8 %shard_map.122 = (bf16[192,384]{1,0:T(8,128)(2,1)}, bf16[192,384]{1,0:T(8,128)(2,1)}, bf16[192,384]{1,0:T(8,128)(2,1)}) custom-call(s32[4]{0:T(128)} %lengths.1, s32[4,16]{1,0:T(4,128)} %table.1, bf16[192,384]{1,0:T(8,128)(2,1)} %get-tuple-element.9.q_hbm, bf16[192,384]{1,0:T(8,128)(2,1)} %get-tuple-element.10.k_hbm, ...), custom_call_target="tpu_custom_call" | custom-call | tf_op jit(solution)/shard_map/pallas_call | solution.py:191

commit v7 on v6

--- a/solution.py
+++ b/solution.py
@@ -16,12 +16,12 @@
 
 
 def attention_kernel(
-    lengths, table, q_hbm, k_hbm, v_hbm, key_pool, value_pool, out_hbm, nk_hbm, nv_hbm,
-    q_ref, k_ref, v_ref, out_ref, kbuf, vbuf, queries, scores, peaks, offsets, totals, mixed, work, sems, io,
+    lengths, table, q_ref, k_ref, v_ref, key_pool, value_pool, out_hbm, nk_hbm, nv_hbm,
+    out_ref, queries, scores, peaks, offsets, totals, mixed, work, io,
 ):
     f32, bf16 = jnp.float32, jnp.bfloat16
     req_count, maxp = table.shape
-    page, width = kbuf.shape[1], kbuf.shape[2]
+    page, width = key_pool.shape[1], key_pool.shape[2]
     fresh = q_ref.shape[0] // req_count
     heads = width // HEAD
     rows = heads * fresh
@@ -29,13 +29,6 @@
     factor = math.log2(math.e) / math.sqrt(HEAD)
     low = -1e30
 
-    loads = [
-        pltpu.make_async_copy(source, target, io.at[n])
-        for n, (source, target) in enumerate(((q_hbm, q_ref), (k_hbm, k_ref), (v_hbm, v_ref)))
-    ]
-    for copy in loads:
-        copy.start()
-
     count = 0
     for r in range(req_count):
         chunks = (lengths[r] + (span - 1)) // span
@@ -45,25 +38,18 @@
             i = count + n
             work[0, i] = r
             work[1, i] = n
-            for p in range(CHUNK_PAGES):
-                number, slot = table[r, n * CHUNK_PAGES + p], i * CHUNK_PAGES + p
-                pltpu.make_async_copy(key_pool.at[number], kbuf.at[slot], sems.at[0, i]).start()
-                pltpu.make_async_copy(value_pool.at[number], vbuf.at[slot], sems.at[1, i]).start()
 
         count = count + chunks
 
-    def pages(i):
-        return pl.ds(i * CHUNK_PAGES, CHUNK_PAGES)
-
-    def wait(pool, buffer, kind, i):
-        pltpu.make_async_copy(pool.at[pl.ds(0, CHUNK_PAGES)], buffer.at[pages(i)], sems.at[kind, i]).wait()
-
-    for copy in loads:
-        copy.wait()
+    def chunk(pool, i):
+        r, n = work[0, i], work[1, i]
+        pages = [pool[table[r, n * CHUNK_PAGES + p]] for p in range(CHUNK_PAGES)]
+        return jnp.concatenate(pages, axis=0)
+
     stores = [
-        pltpu.make_async_copy(k_ref, nk_hbm, io.at[3]),
-        pltpu.make_async_copy(v_ref, nv_hbm, io.at[4]),
-        pltpu.make_async_copy(out_ref, out_hbm, io.at[5]),
+        pltpu.make_async_copy(k_ref, nk_hbm, io.at[0]),
+        pltpu.make_async_copy(v_ref, nv_hbm, io.at[1]),
+        pltpu.make_async_copy(out_ref, out_hbm, io.at[2]),
     ]
     stores[0].start()
     stores[1].start()
@@ -121,12 +107,10 @@
             step((count - 1,))
 
     def first(chunks):
-        for i in chunks:
-            wait(key_pool, kbuf, 0, i)
         values = []
         for i in chunks:
             r, n = work[0, i], work[1, i]
-            keys = kbuf[pages(i)].reshape(span, width)
+            keys = chunk(key_pool, i)
             value = times_keys(queries[r], keys)
             values.append(value + jnp.where(column < lengths[r] - n * span, 0.0, low))
         for i, value in zip(chunks, values):
@@ -146,12 +130,10 @@
         fresh_totals.append(jnp.sum(weights, axis=1, keepdims=True))
 
     def second(chunks):
-        for i in chunks:
-            wait(value_pool, vbuf, 1, i)
         parts = []
         for i in chunks:
             r = work[0, i]
-            values = vbuf[pages(i)].reshape(span, width)
+            values = chunk(value_pool, i)
             offset = jnp.concatenate([offsets[r]] * (span // 128), axis=1)
             weights = jnp.exp2(scores[i] * factor - offset)
             part = times_values(weights, values)
@@ -181,25 +163,20 @@
     rows, width = q.shape
     page = key_pool.shape[1]
     req_count, maxp = table.shape
-    slots = req_count * maxp
-    chunks = slots // CHUNK_PAGES
+    chunks = req_count * maxp // CHUNK_PAGES
     wide = width // HEAD * (rows // req_count)
     f32, bf16 = jnp.float32, jnp.bfloat16
     out = jax.ShapeDtypeStruct((rows, width), bf16)
     smem = pl.BlockSpec(memory_space=pltpu.SMEM)
+    vmem = pl.BlockSpec(memory_space=pltpu.VMEM)
     anywhere = pl.BlockSpec(memory_space=pl.ANY)
     return pl.pallas_call(
         attention_kernel,
         out_shape=(out, out, out),
-        in_specs=[smem, smem] + [anywhere] * 5,
+        in_specs=[smem, smem] + [vmem] * 5,
         out_specs=(anywhere, anywhere, anywhere),
         scratch_shapes=[
             pltpu.VMEM((rows, width), bf16),
-            pltpu.VMEM((rows, width), bf16),
-            pltpu.VMEM((rows, width), bf16),
-            pltpu.VMEM((rows, width), bf16),
-            pltpu.VMEM((slots, page, width), bf16),
-            pltpu.VMEM((slots, page, width), bf16),
             pltpu.VMEM((req_count, wide, 256), bf16),
             pltpu.VMEM((chunks, wide, CHUNK_PAGES * page), f32),
             pltpu.VMEM((req_count, wide, 128), f32),
@@ -207,10 +184,9 @@
             pltpu.VMEM((req_count, wide, 128), f32),
             pltpu.VMEM((req_count, wide, 256), f32),
             pltpu.SMEM((2, chunks), jnp.int32),
-            pltpu.SemaphoreType.DMA((2, chunks)),
-            pltpu.SemaphoreType.DMA((6,)),
+            pltpu.SemaphoreType.DMA((3,)),
         ],
-        compiler_params=pltpu.CompilerParams(vmem_limit_bytes=VMEM_BYTES),
+        compiler_params=pltpu.CompilerParams(vmem_limit_bytes=30 << 20),
     )(lengths, table, q, k, v, key_pool, value_pool)
 
 
@@ -261,8 +237,8 @@
 
 
 def project_kernel(
-    lengths_hbm, x_hbm, w_hbm, group_hbm, gain_hbm, bias_hbm, col_bias_hbm, q_hbm, k_hbm, v_hbm,
-    lengths, x_ref, w_ref, group_ref, gain_ref, bias_ref, col_bias_ref, q_ref, k_ref, v_ref, weights, slabs, normed, acc, cosines, sines, pivot, sums, squares, gains, biases,
+    lengths_hbm, x_hbm, w_hbm, group_hbm, gain_hbm, bias_hbm, col_bias_hbm, q_ref, k_ref, v_ref,
+    lengths, x_ref, w_ref, group_ref, gain_ref, bias_ref, col_bias_ref, weights, slabs, normed, acc, cosines, sines, pivot, sums, squares, gains, biases,
     out1, in1, swapped, out2, in2, load, send, recv,
 ):
     f32, bf16, i32 = jnp.float32, jnp.bfloat16, jnp.int32
@@ -611,13 +587,6 @@
                         value = jnp.where(rotated[j] < ROT, value * cosine + near * sine, value)
                     ref[there, j * 128 : (j + 1) * 128] = value.astype(bf16)
 
-    results = [
-        pltpu.make_async_copy(a, b, load.at[n])
-        for n, (a, b) in enumerate(((q_ref, q_hbm), (k_ref, k_hbm), (v_ref, v_hbm)))
-    ]
-    for copy in results:
-        copy.start()
-
     def sent(kind, ref):
         name = ("z", 4, 1, 0) if kind == "z last" else next(n for n in NUMBER if n[0] == kind)
         remote(name, ref, partner).wait_send()
@@ -632,8 +601,6 @@
     sent("swap", in1)
     sent("first", in1.at[pl.ds(0, CHIPS - 1)])
     sent("second", in1.at[pl.ds(0, CHIPS - 1)])
-    for copy in results:
-        copy.wait()
 
 
 def project(lengths, x, w, group_of, gain, bias, col_bias):
@@ -644,6 +611,7 @@
     f32, bf16 = jnp.float32, jnp.bfloat16
     out = jax.ShapeDtypeStruct((tokens, width), bf16)
     anywhere = pl.BlockSpec(memory_space=pl.ANY)
+    vmem = pl.BlockSpec(memory_space=pltpu.VMEM)
     message = pltpu.VMEM((CHIPS, 8, lanes), bf16)
     wide = pltpu.VMEM((tokens, 128), f32)
     copies = pltpu.SemaphoreType.DMA((len(NUMBER),))
@@ -651,7 +619,7 @@
         project_kernel,
         out_shape=(out, out, out),
         in_specs=[anywhere] * 7,
-        out_specs=(anywhere, anywhere, anywhere),
+        out_specs=(vmem, vmem, vmem),
         scratch_shapes=[
             pltpu.SMEM(lengths.shape, jnp.int32),
             pltpu.VMEM((tokens, part), bf16),
@@ -660,9 +628,6 @@
             pltpu.VMEM(gain.shape, bf16),
             pltpu.VMEM(bias.shape, bf16),
             pltpu.VMEM(col_bias.shape, bf16),
-            pltpu.VMEM((tokens, width), bf16),
-            pltpu.VMEM((tokens, width), bf16),
-            pltpu.VMEM((tokens, width), bf16),
             pltpu.VMEM((CHIPS // 2, 4 * depth, cols), bf16),
             pltpu.VMEM((DEPTH, tokens, part), bf16),
             pltpu.VMEM((DEPTH, tokens, part), bf16),
@@ -684,8 +649,9 @@
             copies,
         ],
         compiler_params=pltpu.CompilerParams(
-            collective_id=0, has_side_effects=True, vmem_limit_bytes=VMEM_BYTES
+            collective_id=0, has_side_effects=True, vmem_limit_bytes=40 << 20
         ),
+        cost_estimate=pl.CostEstimate(flops=10**11, bytes_accessed=10**8, transcendentals=0),
     )(lengths, x, w, group_of, gain, bias, col_bias)
 
 
@@ -694,7 +660,8 @@
 ):
     req_count, fresh, part = arrivals.shape
     x = arrivals.reshape(req_count * fresh, part)
-    q, k, v = project(lengths, x, w_qkv, group_of, ln_gain, ln_bias, qkv_bias)
+    operands = (lengths, x, w_qkv, group_of, ln_gain, ln_bias, qkv_bias)
+    q, k, v = project(*(pltpu.with_memory_space_constraint(a, pltpu.HBM) for a in operands))
     outs = attention(lengths, page_table, q, k, v, key_pool, value_pool)
     return tuple(a.reshape(req_count, fresh, -1) for a in outs)
 

time: 65.2 us -> 64 us (0.982)
  Pallas kernels: 64.4 us -> 63.2 us
    pallas_call x1, Pallas kernels: 57.7 us -> 57 us  [project(): pl.pallas_call(project_kernel, out_shape=(out, out, out), in_specs=[anywh...]
where the time goes in v7:
time: 64 us; the launch traced here: 63.9 us
  Pallas kernels  63.2 us (99%)
  between operations  0.71 us (1%)
    pallas_call x1, Pallas kernels, project(): pl.pallas_call(project_kernel, out_shape=(out, out, out), in_specs=[anywh...  57 us
    pallas_call x1, Pallas kernels, attention(): pl.pallas_call(attention_kernel, out_shape=(out, out, out), in_specs=[sme...  6.19 us

profile of v7, /device:TPU:1, one launch (start us, length us, event | category | flops | bytes accessed | tf_op | source)
XLA Modules:
  0.0 63.9 jit_solution(15734564803837921153)
XLA Ops:
  0.6 0.0 copy-start
  0.6 0.0 copy-start.1
  0.7 0.0 copy-start.2
  0.7 0.0 copy-start.3
  0.7 57.0 %shard_map.121 = (bf16[192,384]{1,0:T(8,128)(2,1)S(1)}, bf16[192,384]{1,0:T(8,128)(2,1)S(1)}, bf16[192,384]{1,0:T(8,128)(2,1)S(1)}) custom-call(s32[4]{0:T(128)} %lengths.1, bf16[192,768]{1,0:T(8,128)(2,1)} %bitcast.4, bf16[192,1152]{1,0:T(8,128)(2,1)} %w_hbm.1, s32[128]{0:T(128)} %group_hbm.1, bf16[6144]{0:T(1024)(128)(2,1)} %gain_hbm.1, ...), custom_call_target="tpu_custom_call" | custom-call | flops 99999997952 | bytes 100000000 | tf_op jit(solution)/shard_map/pallas_call | solution.py:618
  57.6 0.0 copy-done
  57.7 0.0 copy-done.1
  57.7 0.0 copy-done.2
  57.7 0.0 copy-done.3
  57.7 6.2 %shard_map.122 = (bf16[192,384]{1,0:T(8,128)(2,1)}, bf16[192,384]{1,0:T(8,128)(2,1)}, bf16[192,384]{1,0:T(8,128)(2,1)}) custom-call(s32[4]{0:T(128)S(1)} %copy-done.3, s32[4,16]{1,0:T(4,128)S(1)} %copy-done.2, bf16[192,384]{1,0:T(8,128)(2,1)S(1)} %get-tuple-element.9.q_ref, bf16[192,384]{1,0:T(8,128)(2,1)S(1)} %get-tuple-element.10.k_ref, ...), custom_call_target="tpu_custom_call" | custom-call | tf_op jit(solution)/shard_map/pallas_call | solution.py:173
Async XLA Ops:
  0.6 57.0 %copy-start = (bf16[40,128,384]{2,1,0:T(8,128)(2,1)S(1)}, bf16[40,128,384]{2,1,0:T(8,128)(2,1)}, u32[]{:S(2)}) copy-start(bf16[40,128,384]{2,1,0:T(8,128)(2,1)} %key_pool.1) | copy-start | bytes 11796484
  0.6 57.0 %copy-start.1 = (bf16[40,128,384]{2,1,0:T(8,128)(2,1)S(1)}, bf16[40,128,384]{2,1,0:T(8,128)(2,1)}, u32[]{:S(2)}) copy-start(bf16[40,128,384]{2,1,0:T(8,128)(2,1)} %value_pool.1) | copy-start | bytes 11796484
  0.7 57.0 %copy-start.2 = (s32[4,16]{1,0:T(4,128)S(1)}, s32[4,16]{1,0:T(4,128)}, u32[]{:S(2)}) copy-start(s32[4,16]{1,0:T(4,128)} %table.1) | copy-start | bytes 772
  0.7 57.0 %copy-start.3 = (s32[4]{0:T(128)S(1)}, s32[4]{0:T(128)}, u32[]{:S(2)}) copy-start(s32[4]{0:T(128)} %lengths.1) | copy-start | bytes 52

commit v8 on v7

--- a/solution.py
+++ b/solution.py
@@ -208,8 +208,11 @@
         names += [("own", h, s) for s in (1, -1)]
         names += [("own on", h, s) for s in (1, -1)]
         names += [("row", h, du, s) for du in OFFSETS for s in (1, -1)]
-        names += [("row on", h, du, s) for du in OFFSETS for s in (1, -1)]
-        names += [("core", h, du, dv) for du in OFFSETS for dv in OFFSETS]
+        names += [("early", h, s) for s in (1, -1)]
+        names += [("row on", h, du, s) for du in OFFSETS[:-1] for s in (1, -1)]
+        names += [("row on", h, 2, s, p) for s in (1, -1) for p in (0, 1)]
+        names += [("core", h, du, dv) for du in OFFSETS for dv in OFFSETS if (du, dv) != (2, 2)]
+        names += [("core", h, 2, 2, s, p) for s in (1, -1) for p in (0, 1)]
     for s in (1, -1):
         names += [("z", k, s, t) for k in (1, 2, 3) for t in range(THIRDS)]
         names += [("z", 4, s, t) for t, _ in last_parts(s)]
@@ -222,7 +225,9 @@
 
 
 def send_number(name):
-    return SENDS.index("z last" if name[:2] == ("z", 4) else name[0])
+    if name[:2] == ("z", 4):
+        return SENDS.index("z last")
+    return SENDS.index("row" if name[0] == "early" else name[0])
 
 
 def arrivals_in_order():
@@ -232,7 +237,8 @@
     order = rows(0) + thirds(1, 0) + [("own on", 0), ("own on", 1)] + thirds(1, 1, 2)
     order += rows(-1) + thirds(2, 0, 1, 2) + rows(1) + thirds(3, 0) + rows_on(0) + thirds(3, 1, 2)
     order += rows(2) + [("z", 4, -1, 1), ("z", 4, 1, 0), ("z", 4, 1, 1), ("z", 4, -1, 2)]
-    order += rows_on(-1) + ["row 0"] + rows_on(1) + ["row -1"] + rows_on(2) + ["row 1", "near 2", "far 2"]
+    order += rows_on(-1) + ["row 0"] + rows_on(1) + ["row -1"]
+    order += [("last", 0), ("last", 1), "row 1", "near 2", "far 2"]
     return order
 
 
@@ -340,10 +346,16 @@
         u, v = (u + du + SIDE) % SIDE, (v + dv + SIDE) % SIDE
         return v * SIDE + u if h == 0 else u * SIDE + v
 
-    def block(h, du, dv, c=core, sub=None):
+    def block(h, du, dv, c=core, start_row=0, count=rows_half):
         pair, row = place(chip_at(h, du, dv), c)
-        row = row + h * rows_half + (0 if sub in (None, 1) else rows_sub)
-        return weights.at[pair, pl.ds(pl.multiple_of(row, 16), rows_half if sub is None else rows_sub), :]
+        row = row + h * rows_half + start_row
+        return weights.at[pair, pl.ds(pl.multiple_of(row, 16), count), :]
+
+    def sub_rows(s, p=None):
+        start_row = 0 if s == 1 else rows_sub
+        if p is None:
+            return start_row, rows_sub
+        return (start_row, rows_sub - 16) if p == 0 else (start_row + rows_sub - 16, 16)
 
     def weight_copy(name):
         kind, h = name[0], name[1]
@@ -351,15 +363,19 @@
             return remote(name, block(h, 0, 0), device(chip_at(h, name[2], 0)))
         if kind == "own on":
             s = name[2]
-            return remote(name, block(h, -s, 0, sub=s), device(chip_at(h, s, 0)))
+            return remote(name, block(h, -s, 0, core, *sub_rows(s)), device(chip_at(h, s, 0)))
+        if kind == "early":
+            return remote(name, block(h, 0, 0, core, 0, 16), device(chip_at(h, 0, name[2])))
         if kind == "row":
             du, s = name[2], name[3]
-            return remote(name, block(h, du, 0), device(chip_at(h, 0, s)))
+            ref = block(h, 0, 0, core, 16, rows_half - 16) if du == 0 else block(h, du, 0)
+            return remote(name, ref, device(chip_at(h, 0, s)))
         if kind == "row on":
             du, s = name[2], name[3]
-            return remote(name, block(h, du, -s, sub=s), device(chip_at(h, 0, s)))
+            return remote(name, block(h, du, -s, core, *sub_rows(*name[3:])), device(chip_at(h, 0, s)))
         du, dv = name[2], name[3]
-        return remote(name, block(h, du, dv), partner)
+        rows = sub_rows(*name[4:]) if len(name) > 4 else ()
+        return remote(name, block(h, du, dv, core, *rows), partner)
 
     def start(*name):
         weight_copy(name).start()
@@ -372,6 +388,9 @@
             start("own", h, s)
     for h in (0, 1):
         start("core", h, 0, 0)
+    for h in (0, 1):
+        for s in (1, -1):
+            start("early", h, s)
 
     a, b = iota((CHIPS * 8, CHIPS * 8), 0), iota((CHIPS * 8, CHIPS * 8), 1)
     loads[2].wait()
@@ -512,7 +531,13 @@
                 normed[w, mine, lanes] = value.reshape(32, 128).astype(bf16)
 
     def from_core(h, du, dv):
-        remote(("core", h, du, dv), block(h, du, dv, c=1 - core), partner).wait_recv()
+        if (du, dv) != (2, 2):
+            remote(("core", h, du, dv), block(h, du, dv, 1 - core), partner).wait_recv()
+            return
+        for s in (1, -1):
+            for p in (0, 1):
+                ref = block(h, 2, 2, 1 - core, *sub_rows(s, p))
+                remote(("core", h, 2, 2, s, p), ref, partner).wait_recv()
 
     def multiply_pair(pair):
         acc[...] += jnp.dot(normed[pair], weights[pair], preferred_element_type=f32)
@@ -546,8 +571,19 @@
         elif event[0] == "row":
             arrive(*event)
             _, h, du, s = event
-            start("row on", h, du, s)
+            if du == 0:
+                arrive("early", h, s)
+            if du == 2:
+                start("row on", h, 2, s, 0)
+                start("row on", h, 2, s, 1)
+            else:
+                start("row on", h, du, s)
             start("core", h, du, -s)
+        elif event[0] == "last":
+            for h in (1, 0):
+                for s in (1, -1):
+                    arrive("row on", h, 2, s, event[1])
+                    start("core", h, 2, 2, s, event[1])
         elif event[0] == "row on":
             _, h, du = event
             arrive("row on", h, du, 1)

time: 64 us -> 63.9 us (level)
  no operation moved by 1% of the time
where the time goes in v8:
time: 63.9 us; the launch traced here: 63.8 us
  Pallas kernels  63.1 us (99%)
  between operations  0.71 us (1%)
    pallas_call x1, Pallas kernels, project(): pl.pallas_call(project_kernel, out_shape=(out, out, out), in_specs=[anywh...  57.4 us
    pallas_call x1, Pallas kernels, attention(): pl.pallas_call(attention_kernel, out_shape=(out, out, out), in_specs=[sme...  5.63 us

profile of v8, /device:TPU:1, one launch (start us, length us, event | category | flops | bytes accessed | tf_op | source)
XLA Modules:
  0.0 63.8 jit_solution(8811228841282580396)
XLA Ops:
  0.6 0.0 copy-start
  0.6 0.0 copy-start.1
  0.7 0.0 copy-start.2
  0.7 0.0 copy-start.3
  0.7 57.4 %shard_map.121 = (bf16[192,384]{1,0:T(8,128)(2,1)S(1)}, bf16[192,384]{1,0:T(8,128)(2,1)S(1)}, bf16[192,384]{1,0:T(8,128)(2,1)S(1)}) custom-call(s32[4]{0:T(128)} %lengths.1, bf16[192,768]{1,0:T(8,128)(2,1)} %bitcast.4, bf16[192,1152]{1,0:T(8,128)(2,1)} %w_hbm.1, s32[128]{0:T(128)} %group_hbm.1, bf16[6144]{0:T(1024)(128)(2,1)} %gain_hbm.1, ...), custom_call_target="tpu_custom_call" | custom-call | flops 99999997952 | bytes 100000000 | tf_op jit(solution)/shard_map/pallas_call | solution.py:654
  58.1 0.0 copy-done
  58.1 0.0 copy-done.1
  58.1 0.0 copy-done.2
  58.1 0.0 copy-done.3
  58.1 5.6 %shard_map.122 = (bf16[192,384]{1,0:T(8,128)(2,1)}, bf16[192,384]{1,0:T(8,128)(2,1)}, bf16[192,384]{1,0:T(8,128)(2,1)}) custom-call(s32[4]{0:T(128)S(1)} %copy-done.3, s32[4,16]{1,0:T(4,128)S(1)} %copy-done.2, bf16[192,384]{1,0:T(8,128)(2,1)S(1)} %get-tuple-element.9.q_ref, bf16[192,384]{1,0:T(8,128)(2,1)S(1)} %get-tuple-element.10.k_ref, ...), custom_call_target="tpu_custom_call" | custom-call | tf_op jit(solution)/shard_map/pallas_call | solution.py:173
Async XLA Ops:
  0.6 57.5 %copy-start = (bf16[40,128,384]{2,1,0:T(8,128)(2,1)S(1)}, bf16[40,128,384]{2,1,0:T(8,128)(2,1)}, u32[]{:S(2)}) copy-start(bf16[40,128,384]{2,1,0:T(8,128)(2,1)} %key_pool.1) | copy-start | bytes 11796484
  0.6 57.5 %copy-start.1 = (bf16[40,128,384]{2,1,0:T(8,128)(2,1)S(1)}, bf16[40,128,384]{2,1,0:T(8,128)(2,1)}, u32[]{:S(2)}) copy-start(bf16[40,128,384]{2,1,0:T(8,128)(2,1)} %value_pool.1) | copy-start | bytes 11796484
  0.7 57.5 %copy-start.2 = (s32[4,16]{1,0:T(4,128)S(1)}, s32[4,16]{1,0:T(4,128)}, u32[]{:S(2)}) copy-start(s32[4,16]{1,0:T(4,128)} %table.1) | copy-start | bytes 772
  0.7 57.5 %copy-start.3 = (s32[4]{0:T(128)S(1)}, s32[4]{0:T(128)}, u32[]{:S(2)}) copy-start(s32[4]{0:T(128)} %lengths.1) | copy-start | bytes 52

commit v9 on v7

--- a/solution.py
+++ b/solution.py
@@ -49,7 +49,6 @@
     stores = [
         pltpu.make_async_copy(k_ref, nk_hbm, io.at[0]),
         pltpu.make_async_copy(v_ref, nv_hbm, io.at[1]),
-        pltpu.make_async_copy(out_ref, out_hbm, io.at[2]),
     ]
     stores[0].start()
     stores[1].start()
@@ -152,9 +151,11 @@
         high_pair = part[2 * fresh : 3 * fresh] + part[3 * fresh :]
         middle = low_pair[:, 128:] + high_pair[:, :128]
         value = jnp.concatenate([low_pair[:, :128], middle, high_pair[:, 128:]], axis=1)
-        out_ref[pl.ds(r * fresh, fresh), :] = value.astype(out_ref.dtype)
-
-    stores[2].start()
+        mine = pl.ds(r * fresh, fresh)
+        out_ref[mine, :] = value.astype(out_ref.dtype)
+        stores.append(pltpu.make_async_copy(out_ref.at[mine, :], out_hbm.at[mine, :], io.at[2 + r]))
+        stores[-1].start()
+
     for copy in stores:
         copy.wait()
 
@@ -184,7 +185,7 @@
             pltpu.VMEM((req_count, wide, 128), f32),
             pltpu.VMEM((req_count, wide, 256), f32),
             pltpu.SMEM((2, chunks), jnp.int32),
-            pltpu.SemaphoreType.DMA((3,)),
+            pltpu.SemaphoreType.DMA((2 + req_count,)),
         ],
         compiler_params=pltpu.CompilerParams(vmem_limit_bytes=30 << 20),
     )(lengths, table, q, k, v, key_pool, value_pool)

time: 64 us -> 64.2 us (level)
  no operation moved by 1% of the time
where the time goes in v9:
time: 64.2 us; the launch traced here: 64.1 us
  Pallas kernels  63.4 us (99%)
  between operations  0.71 us (1%)
    pallas_call x1, Pallas kernels, project(): pl.pallas_call(project_kernel, out_shape=(out, out, out), in_specs=[anywh...  57 us
    pallas_call x1, Pallas kernels, attention(): pl.pallas_call(attention_kernel, out_shape=(out, out, out), in_specs=[sme...  6.42 us

profile of v9, /device:TPU:1, one launch (start us, length us, event | category | flops | bytes accessed | tf_op | source)
XLA Modules:
  0.0 64.1 jit_solution(12336777988801970340)
XLA Ops:
  0.6 0.0 copy-start
  0.6 0.0 copy-start.1
  0.7 0.0 copy-start.2
  0.7 0.0 copy-start.3
  0.7 57.0 %shard_map.121 = (bf16[192,384]{1,0:T(8,128)(2,1)S(1)}, bf16[192,384]{1,0:T(8,128)(2,1)S(1)}, bf16[192,384]{1,0:T(8,128)(2,1)S(1)}) custom-call(s32[4]{0:T(128)} %lengths.1, bf16[192,768]{1,0:T(8,128)(2,1)} %bitcast.4, bf16[192,1152]{1,0:T(8,128)(2,1)} %w_hbm.1, s32[128]{0:T(128)} %group_hbm.1, bf16[6144]{0:T(1024)(128)(2,1)} %gain_hbm.1, ...), custom_call_target="tpu_custom_call" | custom-call | flops 99999997952 | bytes 100000000 | tf_op jit(solution)/shard_map/pallas_call | solution.py:619
  57.6 0.0 copy-done
  57.7 0.0 copy-done.1
  57.7 0.0 copy-done.2
  57.7 0.0 copy-done.3
  57.7 6.4 %shard_map.122 = (bf16[192,384]{1,0:T(8,128)(2,1)}, bf16[192,384]{1,0:T(8,128)(2,1)}, bf16[192,384]{1,0:T(8,128)(2,1)}) custom-call(s32[4]{0:T(128)S(1)} %copy-done.3, s32[4,16]{1,0:T(4,128)S(1)} %copy-done.2, bf16[192,384]{1,0:T(8,128)(2,1)S(1)} %get-tuple-element.9.q_ref, bf16[192,384]{1,0:T(8,128)(2,1)S(1)} %get-tuple-element.10.k_ref, ...), custom_call_target="tpu_custom_call" | custom-call | tf_op jit(solution)/shard_map/pallas_call | solution.py:174
Async XLA Ops:
  0.6 57.0 %copy-start = (bf16[40,128,384]{2,1,0:T(8,128)(2,1)S(1)}, bf16[40,128,384]{2,1,0:T(8,128)(2,1)}, u32[]{:S(2)}) copy-start(bf16[40,128,384]{2,1,0:T(8,128)(2,1)} %key_pool.1) | copy-start | bytes 11796484
  0.6 57.0 %copy-start.1 = (bf16[40,128,384]{2,1,0:T(8,128)(2,1)S(1)}, bf16[40,128,384]{2,1,0:T(8,128)(2,1)}, u32[]{:S(2)}) copy-start(bf16[40,128,384]{2,1,0:T(8,128)(2,1)} %value_pool.1) | copy-start | bytes 11796484
  0.7 57.0 %copy-start.2 = (s32[4,16]{1,0:T(4,128)S(1)}, s32[4,16]{1,0:T(4,128)}, u32[]{:S(2)}) copy-start(s32[4,16]{1,0:T(4,128)} %table.1) | copy-start | bytes 772
  0.7 57.0 %copy-start.3 = (s32[4]{0:T(128)S(1)}, s32[4]{0:T(128)}, u32[]{:S(2)}) copy-start(s32[4]{0:T(128)} %lengths.1) | copy-start | bytes 52

commit v10 on v8

--- a/solution.py
+++ b/solution.py
@@ -208,7 +208,6 @@
         names += [("own", h, s) for s in (1, -1)]
         names += [("own on", h, s) for s in (1, -1)]
         names += [("row", h, du, s) for du in OFFSETS for s in (1, -1)]
-        names += [("early", h, s) for s in (1, -1)]
         names += [("row on", h, du, s) for du in OFFSETS[:-1] for s in (1, -1)]
         names += [("row on", h, 2, s, p) for s in (1, -1) for p in (0, 1)]
         names += [("core", h, du, dv) for du in OFFSETS for dv in OFFSETS if (du, dv) != (2, 2)]
@@ -227,7 +226,7 @@
 def send_number(name):
     if name[:2] == ("z", 4):
         return SENDS.index("z last")
-    return SENDS.index("row" if name[0] == "early" else name[0])
+    return SENDS.index(name[0])
 
 
 def arrivals_in_order():
@@ -364,12 +363,9 @@
         if kind == "own on":
             s = name[2]
             return remote(name, block(h, -s, 0, core, *sub_rows(s)), device(chip_at(h, s, 0)))
-        if kind == "early":
-            return remote(name, block(h, 0, 0, core, 0, 16), device(chip_at(h, 0, name[2])))
         if kind == "row":
             du, s = name[2], name[3]
-            ref = block(h, 0, 0, core, 16, rows_half - 16) if du == 0 else block(h, du, 0)
-            return remote(name, ref, device(chip_at(h, 0, s)))
+            return remote(name, block(h, du, 0), device(chip_at(h, 0, s)))
         if kind == "row on":
             du, s = name[2], name[3]
             return remote(name, block(h, du, -s, core, *sub_rows(*name[3:])), device(chip_at(h, 0, s)))
@@ -388,9 +384,6 @@
             start("own", h, s)
     for h in (0, 1):
         start("core", h, 0, 0)
-    for h in (0, 1):
-        for s in (1, -1):
-            start("early", h, s)
 
     a, b = iota((CHIPS * 8, CHIPS * 8), 0), iota((CHIPS * 8, CHIPS * 8), 1)
     loads[2].wait()
@@ -571,8 +564,6 @@
         elif event[0] == "row":
             arrive(*event)
             _, h, du, s = event
-            if du == 0:
-                arrive("early", h, s)
             if du == 2:
                 start("row on", h, 2, s, 0)
                 start("row on", h, 2, s, 1)

time: 63.9 us -> 63.4 us (level); the launches traced: 63.8 us -> 62.6 us
  Pallas kernels: 63.1 us -> 61.9 us
    pallas_call x1, Pallas kernels: 5.63 us -> 4.83 us  [attention(): pl.pallas_call(attention_kernel, out_shape=(out, out, out), in_specs=[sme...]
where the time goes in v10:
time: 63.4 us; the launch traced here: 62.6 us
  Pallas kernels  61.9 us (98%)
  between operations  0.71 us (1%)
    pallas_call x1, Pallas kernels, project(): pl.pallas_call(project_kernel, out_shape=(out, out, out), in_specs=[anywh...  57.1 us
    pallas_call x1, Pallas kernels, attention(): pl.pallas_call(attention_kernel, out_shape=(out, out, out), in_specs=[sme...  4.83 us

profile of v10, /device:TPU:1, one launch (start us, length us, event | category | flops | bytes accessed | tf_op | source)
XLA Modules:
  0.0 62.6 jit_solution(17276131219917234774)
XLA Ops:
  0.6 0.0 copy-start
  0.6 0.0 copy-start.1
  0.7 0.0 copy-start.2
  0.7 0.0 copy-start.3
  0.7 57.1 %shard_map.121 = (bf16[192,384]{1,0:T(8,128)(2,1)S(1)}, bf16[192,384]{1,0:T(8,128)(2,1)S(1)}, bf16[192,384]{1,0:T(8,128)(2,1)S(1)}) custom-call(s32[4]{0:T(128)} %lengths.1, bf16[192,768]{1,0:T(8,128)(2,1)} %bitcast.4, bf16[192,1152]{1,0:T(8,128)(2,1)} %w_hbm.1, s32[128]{0:T(128)} %group_hbm.1, bf16[6144]{0:T(1024)(128)(2,1)} %gain_hbm.1, ...), custom_call_target="tpu_custom_call" | custom-call | flops 99999997952 | bytes 100000000 | tf_op jit(solution)/shard_map/pallas_call | solution.py:645
  57.7 0.0 copy-done
  57.8 0.0 copy-done.1
  57.8 0.0 copy-done.2
  57.8 0.0 copy-done.3
  57.8 4.8 %shard_map.122 = (bf16[192,384]{1,0:T(8,128)(2,1)}, bf16[192,384]{1,0:T(8,128)(2,1)}, bf16[192,384]{1,0:T(8,128)(2,1)}) custom-call(s32[4]{0:T(128)S(1)} %copy-done.3, s32[4,16]{1,0:T(4,128)S(1)} %copy-done.2, bf16[192,384]{1,0:T(8,128)(2,1)S(1)} %get-tuple-element.9.q_ref, bf16[192,384]{1,0:T(8,128)(2,1)S(1)} %get-tuple-element.10.k_ref, ...), custom_call_target="tpu_custom_call" | custom-call | tf_op jit(solution)/shard_map/pallas_call | solution.py:173
Async XLA Ops:
  0.6 57.1 %copy-start = (bf16[40,128,384]{2,1,0:T(8,128)(2,1)S(1)}, bf16[40,128,384]{2,1,0:T(8,128)(2,1)}, u32[]{:S(2)}) copy-start(bf16[40,128,384]{2,1,0:T(8,128)(2,1)} %key_pool.1) | copy-start | bytes 11796484
  0.6 57.1 %copy-start.1 = (bf16[40,128,384]{2,1,0:T(8,128)(2,1)S(1)}, bf16[40,128,384]{2,1,0:T(8,128)(2,1)}, u32[]{:S(2)}) copy-start(bf16[40,128,384]{2,1,0:T(8,128)(2,1)} %value_pool.1) | copy-start | bytes 11796484
  0.7 57.1 %copy-start.2 = (s32[4,16]{1,0:T(4,128)S(1)}, s32[4,16]{1,0:T(4,128)}, u32[]{:S(2)}) copy-start(s32[4,16]{1,0:T(4,128)} %table.1) | copy-start | bytes 772
  0.7 57.1 %copy-start.3 = (s32[4]{0:T(128)S(1)}, s32[4]{0:T(128)}, u32[]{:S(2)}) copy-start(s32[4]{0:T(128)} %lengths.1) | copy-start | bytes 52
